TPU v7x, 32 devices: a whole 2x2x4 slice. The times are simulated.
32 devices in a mesh: chan: 4 (over z), tblk: 8 (over y, x, core).
Axes of the slice: x: 2, y: 2, z: 4, core: 2. Of those that a mesh axis runs over, the one named last changes fastest.
Arguments:
- sky_image: float32 [4, 512, 1024], P(None, 'tblk', 'chan'), may hold values from 0 to 2
- dual_coefs: float32 [9, 4, 512, 1024], P(None, None, 'tblk', 'chan'), may hold values from -3 to 3
- phase_screen: float32 [4, 8, 512, 1024], P('chan', 'tblk'), may hold values from -3.140625 to 3.140625
- grid_rows: int32 [4, 8, 64], P('chan', 'tblk'), may hold values from 0 to 511
- grid_weight: float32 [4, 8, 1024, 256], P('chan', 'tblk'), may hold values from -0.1875 to 0.1875
- visibilities: float32 [4, 8, 2, 64, 256], P('chan', 'tblk'), may hold values from -6 to 6
- filters: float32 [9, 2, 3], replicated, may hold values from -1 to 1
- level_counts: int32 [9], replicated, may hold values from 1 to 3, as said below
- radius: float32 [9], replicated, may hold values from 0.5 to 4
Outputs:
- sky_update: float32 [4, 512, 1024], P(None, 'tblk', 'chan')
- dual_update: float32 [9, 4, 512, 1024], P(None, None, 'tblk', 'chan')
Inputs may be any that keep to these rules, and one draw needn't show every extreme that they name: `level_counts`: at least one basis has 3 levels.
All inputs are finite; a program needn't handle non-finite values.
Results may differ from a plain program's by a relative error of at most 0.00011.
Values sent between devices are 32-bit elements; how exact they have to be, the bound alone decides.
A program may use at most 128 MiB of HBM per device.

v0:
```python
import math

import jax
import jax.numpy as jnp
from jax import lax
from jax.sharding import PartitionSpec as P

NBASIS = 9
ITERS = 2
HALO = 4


FULL_PRECISION = lax.Precision.HIGHEST
STEP_PRIMAL = 0.5
STEP_DUAL = 0.5


def shifted(block, axis, distance):
    devices = range(lax.axis_size(axis))
    route = [(i - distance, i) for i in devices if i - distance in devices]
    return lax.ppermute(block, axis, route)


def padded_2(block, sides, width):
    for axis, dim in sides:
        count = lax.axis_size(axis)
        forward = [(i, i + 1) for i in range(count - 1)]
        backward = [(target, source) for source, target in forward]
        low = lax.ppermute(
            lax.slice_in_dim(block, block.shape[dim] - width, None, axis=dim), axis, forward
        )
        high = lax.ppermute(lax.slice_in_dim(block, 0, width, axis=dim), axis, backward)
        block = jnp.concatenate([low, block, high], axis=dim)
    return block


def product(form, left, right):
    return jnp.einsum(
        form, left, right, precision=FULL_PRECISION, preferred_element_type=jnp.float32
    )


def filter_forward(padded, filter_taps, stride, rows_out, cols_out):
    across = jnp.zeros(padded.shape[:2] + (cols_out,), jnp.float32)
    for offset in (-1, 0, 1):
        first_col = HALO + offset * stride
        across = across + filter_taps[1, offset + 1] * lax.dynamic_slice_in_dim(
            padded, first_col, cols_out, 2
        )
    result = jnp.zeros((padded.shape[0], rows_out, cols_out), jnp.float32)
    for offset in (-1, 0, 1):
        first_row = HALO + offset * stride
        result = result + filter_taps[0, offset + 1] * lax.dynamic_slice_in_dim(
            across, first_row, rows_out, 1
        )
    return result


def filter_back(padded, filter_taps, stride, rows_out, cols_out):
    across = jnp.zeros(padded.shape[:2] + (cols_out,), jnp.float32)
    for offset in (-1, 0, 1):
        first_col = HALO - offset * stride
        across = across + filter_taps[1, offset + 1] * lax.dynamic_slice_in_dim(
            padded, first_col, cols_out, 2
        )
    result = jnp.zeros((padded.shape[0], rows_out, cols_out), jnp.float32)
    for offset in (-1, 0, 1):
        first_row = HALO - offset * stride
        result = result + filter_taps[0, offset + 1] * lax.dynamic_slice_in_dim(
            across, first_row, rows_out, 1
        )
    return result


def per_device(
    sky_image,
    dual_coefs,
    phase_screen,
    grid_rows,
    grid_weight,
    visibilities,
    filters,
    level_counts,
    radius,
):
    channels = sky_image.shape[0]
    facet_rows = sky_image.shape[1]
    facet_cols = sky_image.shape[2]
    full_rows = facet_rows * lax.axis_size("tblk")
    full_cols = phase_screen.shape[3]
    screen = jnp.transpose(phase_screen[:, 0], (1, 0, 2))
    cos_screen = jnp.cos(screen)
    sin_screen = jnp.sin(screen)
    weight = grid_weight[:, 0]
    data_real = visibilities[:, 0, 0]
    data_imag = visibilities[:, 0, 1]
    col_index = jnp.arange(full_cols, dtype=jnp.int32)
    col_angle = (col_index[:, None] * col_index[None, :] % full_cols).astype(jnp.float32) * (
        2.0 * math.pi / full_cols
    )
    cols_real = jnp.cos(col_angle) / math.sqrt(full_cols)
    cols_imag = -jnp.sin(col_angle) / math.sqrt(full_cols)
    row_index = jnp.arange(full_rows, dtype=jnp.int32)
    row_angle = (grid_rows[:, 0][:, :, None] * row_index[None, None, :] % full_rows).astype(
        jnp.float32
    ) * (2.0 * math.pi / full_rows)
    rows_real = jnp.cos(row_angle) / math.sqrt(full_rows)
    rows_imag = -jnp.sin(row_angle) / math.sqrt(full_rows)
    spacing = lax.shift_left(jnp.ones_like(level_counts), level_counts - 1)
    radius_cells = radius[:, None, None, None]
    current = sky_image
    dual_now = dual_coefs
    for sweep_index in range(ITERS):
        spread = lax.all_to_all(current, "chan", split_axis=0, concat_axis=2, tiled=True)
        image_strip = jnp.transpose(spread, (1, 0, 2))
        whole_image = lax.all_gather(image_strip, "tblk", axis=0, tiled=True)
        screened_real = cos_screen * whole_image
        screened_imag = sin_screen * whole_image
        spec_real = product("crk,kcl->crl", rows_real, screened_real) - product(
            "crk,kcl->crl", rows_imag, screened_imag
        )
        spec_imag = product("crk,kcl->crl", rows_real, screened_imag) + product(
            "crk,kcl->crl", rows_imag, screened_real
        )
        sky_real = product("crl,lm->crm", spec_real, cols_real) - product(
            "crl,lm->crm", spec_imag, cols_imag
        )
        sky_imag = product("crl,lm->crm", spec_real, cols_imag) + product(
            "crl,lm->crm", spec_imag, cols_real
        )
        misfit_real = product("crm,cmv->crv", sky_real, weight) - data_real
        misfit_imag = product("crm,cmv->crv", sky_imag, weight) - data_imag
        gridded_real = product("crv,cmv->crm", misfit_real, weight)
        gridded_imag = product("crv,cmv->crm", misfit_imag, weight)
        gradient_back_real = product("crm,ml->crl", gridded_real, cols_real) + product(
            "crm,ml->crl", gridded_imag, cols_imag
        )
        gradient_back_imag = product("crm,ml->crl", gridded_imag, cols_real) - product(
            "crm,ml->crl", gridded_real, cols_imag
        )
        grid_real = product("crk,crl->kcl", rows_real, gradient_back_real) + product(
            "crk,crl->kcl", rows_imag, gradient_back_imag
        )
        grid_imag = product("crk,crl->kcl", rows_real, gradient_back_imag) - product(
            "crk,crl->kcl", rows_imag, gradient_back_real
        )
        summed = lax.psum_scatter(
            cos_screen * grid_real + sin_screen * grid_imag, "tblk", scatter_dimension=0, tiled=True
        )
        gradient = lax.all_to_all(
            jnp.transpose(summed, (1, 0, 2)), "chan", split_axis=2, concat_axis=0, tiled=True
        )
        padded = jnp.pad(dual_now, ((0, 0), (0, 0), (2 * HALO, 2 * HALO), (2 * HALO, 2 * HALO)))
        widened = jnp.zeros((channels, facet_rows + 2 * HALO, facet_cols + 2 * HALO), jnp.float32)
        for synthesis_basis_index in range(NBASIS):
            widened = widened + filter_back(
                padded[synthesis_basis_index],
                filters[synthesis_basis_index],
                spacing[synthesis_basis_index],
                facet_rows + 2 * HALO,
                facet_cols + 2 * HALO,
            )
        from_left = shifted(widened[:, :, facet_cols + HALO :], "chan", 1)
        from_right = shifted(widened[:, :, :HALO], "chan", -1)
        middle = widened[:, :, HALO : HALO + facet_cols]
        middle = (
            middle
            + jnp.pad(from_left, ((0, 0), (0, 0), (0, facet_cols - HALO)))
            + jnp.pad(from_right, ((0, 0), (0, 0), (facet_cols - HALO, 0)))
        )
        from_above = shifted(middle[:, facet_rows + HALO :], "tblk", 1)
        from_below = shifted(middle[:, :HALO], "tblk", -1)
        core = middle[:, HALO : HALO + facet_rows]
        synthesised = (
            core
            + jnp.pad(from_above, ((0, 0), (0, facet_rows - HALO), (0, 0)))
            + jnp.pad(from_below, ((0, 0), (facet_rows - HALO, 0), (0, 0)))
        )
        updated = jnp.maximum(current - STEP_PRIMAL * (gradient + synthesised), 0.0)
        leading = 2.0 * updated - current
        extended = padded_2(leading, (("chan", 2), ("tblk", 1)), HALO)
        coefficients = jnp.stack(
            [
                filter_forward(
                    extended, filters[basis_index], spacing[basis_index], facet_rows, facet_cols
                )
                for basis_index in range(NBASIS)
            ]
        )
        raised = dual_now + STEP_DUAL * coefficients
        norm_cells = jnp.sqrt(jnp.sum(raised * raised, axis=1, keepdims=True))
        dual_now = raised * radius_cells / jnp.maximum(norm_cells, radius_cells)
        current = updated
    return (current, dual_now)


def solution(mesh):
    placed = (
        P(None, "tblk", "chan"),
        P(None, None, "tblk", "chan"),
        P("chan", "tblk", None, None),
        P("chan", "tblk", None),
        P("chan", "tblk", None, None),
        P("chan", "tblk", None, None, None),
        P(),
        P(),
        P(),
    )
    return jax.shard_map(
        per_device,
        mesh=mesh,
        in_specs=placed,
        out_specs=(P(None, "tblk", "chan"), P(None, None, "tblk", "chan")),
        check_vma=False,
    )
```

profile of v0, /device:TPU:11, one launch (start us, length us, event | category | flops | bytes accessed | tf_op | source)
XLA Modules:
  0.0 810.9 jit_solution(2160641394983168815)
XLA Ops:
  7.2 11.1 %all_to_all.66 = f32[4,64,256]{2,1,0:T(8,128)S(1)} all-to-all(f32[4,64,256]{2,1,0:T(8,128)} %param.9), channel_id=1, replica_groups=mesh['chan'=4,'tblk'=8] {'chan'}, dimensions={0} | all-to-all | bytes 524288 | tf_op jit(solution)/shard_map/all_to_all | solution.py:114
  43.1 5.7 pad_slice_fusion.17
  51.8 5.5 fusion.91
  57.4 5.6 fusion.95
  62.9 5.5 fusion.99
  68.5 8.1 fusion.466
  76.5 6.2 copy.51
  82.8 4.9 fusion.16
  93.0 18.5 %fusion.29 = f32[64,1024]{1,0:T(8,128)S(1)} fusion(f32[64,1024]{1,0:T(8,128)S(1)} %fusion.43), kind=kOutput, calls=%fused_computation.66 | convolution fusion | flops 821035008 | bytes 524288 | tf_op jit(solution)/shard_map/crl,lm->crm/dot_general | solution.py:38
  114.1 18.3 %fusion.31 = f32[64,1024]{1,0:T(8,128)S(1)} fusion(f32[64,1024]{1,0:T(8,128)S(1)} %fusion.40), kind=kOutput, calls=%fused_computation.68 | convolution fusion | flops 821035008 | bytes 524288 | tf_op jit(solution)/shard_map/crl,lm->crm/dot_general | solution.py:38
  132.3 18.4 %fusion.53 = f32[64,1024]{1,0:T(8,128)S(1)} fusion(f32[64,1024]{1,0:T(8,128)S(1)} %fusion.29, f32[64,1024]{1,0:T(8,128)S(1)} %fusion.40), kind=kOutput, calls=%fused_computation.82 | convolution fusion | flops 822149120 | bytes 786432 | tf_op jit(solution)/shard_map/crl,lm->crm/dot_general | solution.py:38
  150.7 18.8 %fusion.52 = f32[64,1024]{1,0:T(8,128)S(1)} fusion(f32[64,1024]{1,0:T(8,128)S(1)} %fusion.31, f32[64,1024]{1,0:T(8,128)S(1)} %fusion.43), kind=kOutput, calls=%fused_computation.81 | convolution fusion | flops 822149120 | bytes 786432 | tf_op jit(solution)/shard_map/crl,lm->crm/dot_general | solution.py:38
  173.0 18.3 %fusion.28 = f32[64,1024]{1,0:T(8,128)S(1)} fusion(f32[64,1024]{1,0:T(8,128)S(1)} %fusion.66), kind=kOutput, calls=%fused_computation.65 | convolution fusion | flops 821035008 | bytes 524288 | tf_op jit(solution)/shard_map/crm,ml->crl/dot_general | solution.py:38
  191.3 18.4 %fusion.30 = f32[64,1024]{1,0:T(8,128)S(1)} fusion(f32[64,1024]{1,0:T(8,128)S(1)} %fusion.69), kind=kOutput, calls=%fused_computation.67 | convolution fusion | flops 821035008 | bytes 524288 | tf_op jit(solution)/shard_map/crm,ml->crl/dot_general | solution.py:38
  209.7 18.6 %fusion.55 = f32[64,1024]{1,0:T(8,128)S(1)} fusion(f32[64,1024]{1,0:T(8,128)S(1)} %fusion.28, f32[64,1024]{1,0:T(8,128)S(1)} %fusion.69), kind=kOutput, calls=%fused_computation.84 | convolution fusion | flops 822149120 | bytes 786432 | tf_op jit(solution)/shard_map/crm,ml->crl/dot_general | solution.py:38
  233.0 18.8 %fusion.54 = f32[64,1024]{1,0:T(8,128)S(1)} fusion(f32[64,1024]{1,0:T(8,128)S(1)} %fusion.30, f32[64,1024]{1,0:T(8,128)S(1)} %fusion.66), kind=kOutput, calls=%fused_computation.83 | convolution fusion | flops 822149120 | bytes 786432 | tf_op jit(solution)/shard_map/crm,ml->crl/dot_general | solution.py:38
  254.1 4.3 fusion.7
  258.4 6.1 copy.54
  275.0 6.9 fusion.103
  281.9 19.3 %fusion.136 = f32[4,72,264]{2,1,0:T(8,128)S(1)} fusion(f32[4,80,264]{2,1,0:T(8,128)S(1)} %copy-done.17, f32[4,80,264]{2,1,0:T(8,128)S(1)} %copy-done.18, f32[4,80,264]{2,1,0:T(8,128)S(1)} %copy-done.19, f32[4,80,264]{2,1,0:T(8,128)S(1)} %copy-done.20, f32[4,80,264]{2,1,0:T(8,128)S(1)} %copy-done.21, f32[4,80,264]{2,1,0:T(8,128)S(1)} %copy-done.22, ...), kind=kLoop, calls=%fused_computation.199 | loop fusion | flops 4029696 | bytes 8515764 | tf_op jit(solution)/shard_map/add | solution.py:156
  309.3 17.4 %all-reduce.15.cloned.1.call-done = f32[512,1,1024]{2,1,0:T(1,128)} async-done(((f32[512,1,1024]{2,1,0:T(1,128)}), f32[512,1,1024]{2,1,0:T(1,128)}) %all-reduce.15.cloned.1.call-update) | async-done | bytes 2097168
  329.2 3.7 reduce
  335.0 4.6 all-to-all-start.1
  341.6 4.7 collective-permute-start.2
  356.0 3.1 collective-permute-start.4
  366.5 5.6 collective-permute-start.6
  391.3 4.3 all-to-all-start.2
  396.7 5.9 multiply_add_fusion.15
  407.9 6.2 multiply_add_fusion.13
  416.8 7.1 multiply_add_fusion.11
  438.6 3.9 fusion.210
  442.4 3.8 fusion.206
  451.0 3.3 pad_slice_fusion.8
  454.3 3.0 fusion.89
  457.3 3.1 fusion.73
  460.4 3.1 fusion.75
  463.5 3.1 fusion.77
  466.7 3.1 fusion.79
  472.8 3.1 fusion.83
  475.8 6.2 copy.67
  482.1 4.9 fusion.8
  492.3 18.7 %fusion.25 = f32[64,1024]{1,0:T(8,128)S(1)} fusion(f32[64,1024]{1,0:T(8,128)S(1)} %fusion.49), kind=kOutput, calls=%fused_computation.62 | convolution fusion | flops 821035008 | bytes 524288 | tf_op jit(solution)/shard_map/crl,lm->crm/dot_general | solution.py:38
  513.6 18.3 %fusion.27 = f32[64,1024]{1,0:T(8,128)S(1)} fusion(f32[64,1024]{1,0:T(8,128)S(1)} %fusion.46), kind=kOutput, calls=%fused_computation.64 | convolution fusion | flops 821035008 | bytes 524288 | tf_op jit(solution)/shard_map/crl,lm->crm/dot_general | solution.py:38
  531.8 18.4 %fusion.57 = f32[64,1024]{1,0:T(8,128)S(1)} fusion(f32[64,1024]{1,0:T(8,128)S(1)} %fusion.25, f32[64,1024]{1,0:T(8,128)S(1)} %fusion.46), kind=kOutput, calls=%fused_computation.86 | convolution fusion | flops 822149120 | bytes 786432 | tf_op jit(solution)/shard_map/crl,lm->crm/dot_general | solution.py:38
  550.9 18.5 %fusion.56 = f32[64,1024]{1,0:T(8,128)S(1)} fusion(f32[64,1024]{1,0:T(8,128)S(1)} %fusion.27, f32[64,1024]{1,0:T(8,128)S(1)} %fusion.49), kind=kOutput, calls=%fused_computation.85 | convolution fusion | flops 822149120 | bytes 786432 | tf_op jit(solution)/shard_map/crl,lm->crm/dot_general | solution.py:38
  572.3 18.3 %fusion.24 = f32[64,1024]{1,0:T(8,128)S(1)} fusion(f32[64,1024]{1,0:T(8,128)S(1)} %fusion.60), kind=kOutput, calls=%fused_computation.61 | convolution fusion | flops 821035008 | bytes 524288 | tf_op jit(solution)/shard_map/crm,ml->crl/dot_general | solution.py:38
  590.5 18.5 %fusion.26 = f32[64,1024]{1,0:T(8,128)S(1)} fusion(f32[64,1024]{1,0:T(8,128)S(1)} %fusion.63), kind=kOutput, calls=%fused_computation.63 | convolution fusion | flops 821035008 | bytes 524288 | tf_op jit(solution)/shard_map/crm,ml->crl/dot_general | solution.py:38
  609.0 18.8 %fusion.59 = f32[64,1024]{1,0:T(8,128)S(1)} fusion(f32[64,1024]{1,0:T(8,128)S(1)} %fusion.24, f32[64,1024]{1,0:T(8,128)S(1)} %fusion.63), kind=kOutput, calls=%fused_computation.88 | convolution fusion | flops 822149120 | bytes 786432 | tf_op jit(solution)/shard_map/crm,ml->crl/dot_general | solution.py:38
  632.5 18.5 %fusion.58 = f32[64,1024]{1,0:T(8,128)S(1)} fusion(f32[64,1024]{1,0:T(8,128)S(1)} %fusion.26, f32[64,1024]{1,0:T(8,128)S(1)} %fusion.60), kind=kOutput, calls=%fused_computation.87 | convolution fusion | flops 822149120 | bytes 786432 | tf_op jit(solution)/shard_map/crm,ml->crl/dot_general | solution.py:38
  653.3 4.3 fusion.6
  657.6 6.1 copy.69
  663.8 4.0 fusion.85
  667.9 3.7 fusion.87
  671.6 19.3 %fusion.110 = f32[4,72,264]{2,1,0:T(8,128)S(1)} fusion(f32[4,80,264]{2,1,0:T(8,128)S(1)} %copy-done.11, f32[4,80,264]{2,1,0:T(8,128)S(1)} %copy-done.12, f32[4,80,264]{2,1,0:T(8,128)S(1)} %copy-done.13, f32[4,80,264]{2,1,0:T(8,128)S(1)} %copy-done.14, f32[4,80,264]{2,1,0:T(8,128)S(1)} %copy-done.15, f32[4,80,264]{2,1,0:T(8,128)S(1)} %copy-done.16, ...), kind=kLoop, calls=%fused_computation.164 | loop fusion | flops 4029696 | bytes 8515764 | tf_op jit(solution)/shard_map/add | solution.py:156
  691.8 3.2 collective-permute-start.8
  697.2 27.9 %all-reduce.17.cloned.1.call-done = f32[512,1,1024]{2,1,0:T(1,128)} async-done(((f32[512,1,1024]{2,1,0:T(1,128)}), f32[512,1,1024]{2,1,0:T(1,128)}) %all-reduce.17.cloned.1.call-update) | async-done | bytes 2097168
  729.4 4.6 all-to-all-start.3
  734.2 4.7 collective-permute-start.10
  745.8 3.1 collective-permute-start.12
  755.9 3.2 collective-permute-start.14
  761.0 4.1 collective-permute-done.15
  765.3 6.2 multiply_add_fusion.2
  771.5 6.2 multiply_add_fusion.4
  777.7 5.9 multiply_add_fusion.6
  (208 shorter events, 160.4 us)
Async XLA Ops:
  7.2 162.3 %copy-start = (f32[1,1,1024,256]{3,2,1,0:T(8,128)S(1)}, f32[1,1,1024,256]{3,2,1,0:T(8,128)}, u32[]{:S(2)}) copy-start(f32[1,1,1024,256]{3,2,1,0:T(8,128)} %param.13) | copy-start | bytes 3145732
  7.2 28.9 %copy-start.27 = (f32[1,1,512,1024]{3,2,1,0:T(8,128)S(1)}, f32[1,1,512,1024]{3,2,1,0:T(8,128)}, u32[]{:S(2)}) copy-start(f32[1,1,512,1024]{3,2,1,0:T(8,128)} %param.11) | copy-start | bytes 6291460
  7.2 69.4 %all-gather.3.cloned.1.call-start = ((), (), s32[]{:S(2)}) async-start(), calls=%async_computation.4 | async-start | bytes 2359296 | tf_op jit(solution)/shard_map/all_gather | solution.py:116
  19.5 307.2 %all-reduce.15.cloned.1.call-start = ((), (), s32[]{:S(2)}) async-start(), calls=%async_computation.6 | async-start | bytes 4194304
  62.9 5.5 copy-start.8
  76.5 6.2 copy-start.32
  82.7 5.0 copy-start.1
  82.7 5.0 copy-start.3
  150.7 18.8 %copy-start.29 = (f32[1,1,2,64,256]{4,3,2,1,0:T(8,128)S(1)}, f32[1,1,2,64,256]{4,3,2,1,0:T(8,128)}, u32[]{:S(2)}) copy-start(f32[1,1,2,64,256]{4,3,2,1,0:T(8,128)} %param.14) | copy-start | bytes 393220
  274.9 6.9 copy-start.9
  274.9 6.9 copy-start.17
  274.9 6.9 copy-start.18
  274.9 6.9 copy-start.19
  274.9 6.9 copy-start.20
  274.9 6.9 copy-start.21
  274.9 6.9 copy-start.22
  281.9 26.2 %copy-start.35 = (u32[32]{0:T(128)S(1)}, u32[32]{0:T(128)}, u32[]{:S(2)}) copy-start(u32[32]{0:T(128)} %constant.318) | copy-start | bytes 388
  301.2 0.8 copy-start.25
  302.8 36.8 %collective-permute-start = (f32[4,72,4]{2,1,0:T(8,128)}, f32[4,72,4]{2,1,0:T(8,128)S(1)}, u32[]{:S(2)}, u32[]{:S(2)}) collective-permute-start(f32[4,72,4]{2,1,0:T(8,128)} %get-tuple-element.68), channel_id=1, source_target_pairs={{0,8},{8,16},{16,24},{1,9},{9,17},{17,25},{2,10},{10,18},{18,26},{... | collective-permute-start | bytes 13832 | tf_op jit(solution)/shard_map/ppermute | solution.py:21
  305.7 33.8 %collective-permute-start.1 = (f32[4,72,4]{2,1,0:T(8,128)}, f32[4,72,4]{2,1,0:T(8,128)}, u32[]{:S(2)}, u32[]{:S(2)}) collective-permute-start(f32[4,72,4]{2,1,0:T(8,128)} %get-tuple-element.69), channel_id=1, source_target_pairs={{8,0},{16,8},{24,16},{9,1},{17,9},{25,17},{10,2},{18,10},{26,18},{... | collective-permute-start | bytes 13832 | tf_op jit(solution)/shard_map/ppermute | solution.py:21
  335.0 13.4 %all-to-all-start.1 = ((f32[4,1,16384]{2,1,0:T(1,128)}), f32[4,1,16384]{2,1,0:T(1,128)}, u32[]{:S(2)}, u32[]{:S(2)}) async-start(f32[4,1,16384]{2,1,0:T(1,128)} %reshape.925), calls=%async_computation.1 | async-start | bytes 524288 | tf_op jit(solution)/shard_map/all_to_all | solution.py:150
  340.8 0.7 copy-start.28
  341.6 12.4 %collective-permute-start.2 = (f32[4,4,256]{2,1,0:T(4,128)S(1)}, f32[4,4,256]{2,1,0:T(4,128)S(1)}, u32[]{:S(2)}, u32[]{:S(2)}) collective-permute-start(f32[4,4,256]{2,1,0:T(4,128)S(1)} %get-tuple-element.72), channel_id=1, source_target_pairs={{0,1},{1,2},{2,3},{3,4},{4,5},{5,6},{6,7},{8,9},{9,10},{10,11},{11... | collective-permute-start | bytes 49160 | tf_op jit(solution)/shard_map/ppermute | solution.py:21
  346.3 7.7 collective-permute-start.3
  356.0 6.3 collective-permute-start.4
  359.1 6.0 collective-permute-start.5
  365.1 0.7 copy-start.31
  366.5 29.1 %collective-permute-start.6 = (f32[4,4,264]{2,1,0:T(4,128)}, f32[4,4,264]{2,1,0:T(4,128)}, u32[]{:S(2)}, u32[]{:S(2)}) collective-permute-start(f32[4,4,264]{2,1,0:T(4,128)} %get-tuple-element.46), channel_id=1, source_target_pairs={{0,1},{1,2},{2,3},{3,4},{4,5},{5,6},{6,7},{8,9},{9,10},{10,11},{11... | collective-permute-start | bytes 50696 | tf_op jit(solution)/shard_map/ppermute | solution.py:29
  372.1 23.5 %collective-permute-start.7 = (f32[4,4,264]{2,1,0:T(4,128)}, f32[4,4,264]{2,1,0:T(4,128)}, u32[]{:S(2)}, u32[]{:S(2)}) collective-permute-start(f32[4,4,264]{2,1,0:T(4,128)} %get-tuple-element.47), channel_id=1, source_target_pairs={{1,0},{2,1},{3,2},{4,3},{5,4},{6,5},{7,6},{9,8},{10,9},{11,10},{12... | collective-permute-start | bytes 50696 | tf_op jit(solution)/shard_map/ppermute | solution.py:32
  391.3 40.6 %all-to-all-start.2 = ((f32[4,64,256]{2,1,0:T(8,128)}), f32[4,64,256]{2,1,0:T(8,128)}, u32[]{:S(2)}, u32[]{:S(2)}) async-start(f32[4,64,256]{2,1,0:T(8,128)} %get-tuple-element.5), calls=%async_computation.2 | async-start | bytes 524288 | tf_op jit(solution)/shard_map/all_to_all | solution.py:114
  395.6 80.2 %all-gather.5.cloned.1.call-start = ((), (), s32[]{:S(2)}) async-start(), calls=%async_computation.5 | async-start | bytes 2359296 | tf_op jit(solution)/shard_map/all_gather | solution.py:116
  435.7 289.5 %all-reduce.17.cloned.1.call-start = ((), (), s32[]{:S(2)}) async-start(), calls=%async_computation.7 | async-start | bytes 4194304
  435.7 10.5 %copy-start.7 = (f32[9,4,64,256]{3,2,1,0:T(8,128)S(1)}, f32[9,4,64,256]{3,2,1,0:T(8,128)}, u32[]{:S(2)}) copy-start(f32[9,4,64,256]{3,2,1,0:T(8,128)} %param.10) | copy-start | bytes 7077892
  446.3 2.3 copy-start.34
  451.0 3.3 copy-start.5
  475.8 6.2 copy-start.33
  482.1 5.0 copy-start.2
  482.1 5.0 copy-start.4
  531.8 18.4 %copy-start.30 = (f32[1,1,2,64,256]{4,3,2,1,0:T(8,128)S(1)}, f32[1,1,2,64,256]{4,3,2,1,0:T(8,128)}, u32[]{:S(2)}) copy-start(f32[1,1,2,64,256]{4,3,2,1,0:T(8,128)} %param.14) | copy-start | bytes 393220
  663.7 7.8 copy-start.10
  663.7 7.8 copy-start.11
  663.8 7.8 copy-start.12
  663.8 7.8 copy-start.13
  663.8 7.8 copy-start.14
  663.8 7.8 copy-start.15
  663.8 7.8 copy-start.16
  690.9 0.8 copy-start.23
  691.8 42.2 %copy-start.24 = (f32[4,72,264]{2,1,0:T(8,128)S(1)}, f32[4,72,264]{2,1,0:T(8,128)}, u32[]{:S(2)}) copy-start(f32[4,72,264]{2,1,0:T(8,128)} %copy-done.23) | copy-start | bytes 912388
  691.8 42.2 %collective-permute-start.8 = (f32[4,72,4]{2,1,0:T(8,128)S(1)}, f32[4,72,4]{2,1,0:T(8,128)S(1)}, u32[]{:S(2)}, u32[]{:S(2)}) collective-permute-start(f32[4,72,4]{2,1,0:T(8,128)S(1)} %get-tuple-element.57), channel_id=1, source_target_pairs={{0,8},{8,16},{16,24},{1,9},{9,17},{17,25},{2,10},{10,18},{18,26},{... | collective-permute-start | bytes 13832 | tf_op jit(solution)/shard_map/ppermute | solution.py:21
  695.0 39.0 %collective-permute-start.9 = (f32[4,72,4]{2,1,0:T(8,128)S(1)}, f32[4,72,4]{2,1,0:T(8,128)S(1)}, u32[]{:S(2)}, u32[]{:S(2)}) collective-permute-start(f32[4,72,4]{2,1,0:T(8,128)S(1)} %get-tuple-element.58), channel_id=1, source_target_pairs={{8,0},{16,8},{24,16},{9,1},{17,9},{25,17},{10,2},{18,10},{26,18},{... | collective-permute-start | bytes 13832 | tf_op jit(solution)/shard_map/ppermute | solution.py:21
  728.4 16.5 %copy-start.26 = (f32[4,64,256]{2,1,0:T(8,128)S(1)}, f32[4,64,256]{2,1,0:T(8,128)}, u32[]{:S(2)}) copy-start(f32[4,64,256]{2,1,0:T(8,128)} %get-tuple-element.5) | copy-start | bytes 786436
  729.4 11.7 %all-to-all-start.3 = ((f32[4,1,16384]{2,1,0:T(1,128)}), f32[4,1,16384]{2,1,0:T(1,128)S(1)}, u32[]{:S(2)}, u32[]{:S(2)}) async-start(f32[4,1,16384]{2,1,0:T(1,128)} %reshape.927), calls=%async_computation.3 | async-start | bytes 524288 | tf_op jit(solution)/shard_map/all_to_all | solution.py:150
  734.2 9.0 %collective-permute-start.10 = (f32[4,4,256]{2,1,0:T(4,128)S(1)}, f32[4,4,256]{2,1,0:T(4,128)S(1)}, u32[]{:S(2)}, u32[]{:S(2)}) collective-permute-start(f32[4,4,256]{2,1,0:T(4,128)S(1)} %get-tuple-element.70), channel_id=1, source_target_pairs={{0,1},{1,2},{2,3},{3,4},{4,5},{5,6},{6,7},{8,9},{9,10},{10,11},{11... | collective-permute-start | bytes 49160 | tf_op jit(solution)/shard_map/ppermute | solution.py:21
  738.9 6.0 collective-permute-start.11
  745.8 7.4 collective-permute-start.12
  748.9 6.9 collective-permute-start.13
  755.9 5.1 collective-permute-start.14
  759.0 6.0 collective-permute-start.15
  793.4 8.0 copy-start.6
Sparse Core Ops, SparseCore 0:
  19.6 30.1 all-gather.2
  264.6 62.0 all-reduce.14
  435.8 29.2 all-gather.4
  663.9 61.2 all-reduce.16
where the time goes:
time: 822 us; the launch traced here: 811 us
  matrix products  351 us (43%)
  other arithmetic  199 us (24%)
  local copies, waits for them, and re-layouts  72.9 us (9%)
  starting transfers between devices  61.1 us (7%)
  waiting for transfers between devices  59.7 us (7%)
  between operations  55.8 us (7%)
  blocking collectives  11.1 us (1%)
    dot_general x40, matrix products, product(): jnp.einsum(form, left, right, precision=FULL_PRECISION, preferred_element...  351 us
    add x14, other arithmetic, filter_back(): across + filter_taps[1, offset + 1] * lax.dynamic_slice_in_dim(padded, fi...  55.7 us
    unnamed x6, waiting for transfers between devices  45.4 us
    unnamed x18, other arithmetic  43.9 us
    add x2, other arithmetic, per_device(): widened + filter_back(padded[synthesis_basis_index], filters[synthesis_ba...  38.6 us
    add x6, other arithmetic, filter_forward(): across + filter_taps[1, offset + 1] * lax.dynamic_slice_in_dim(padded, fi...  37.6 us
    ppermute x8, starting transfers between devices, shifted(): return lax.ppermute(block, axis, route)  24.3 us
  transfers between devices with their start and end apart: 23, of which 8 were waited for; matrix products, arithmetic and copies ran while one was open for 24% of the time, Pallas kernels for 0%

commit v1 on v0

v1 whole, which is shorter than its diff:
```python
import functools
import math

import jax
import jax.numpy as jnp
from jax import lax
from jax.experimental import pallas as pl
from jax.experimental.pallas import tpu as pltpu
from jax.sharding import PartitionSpec as P

ITERS = 2
HALO = 4
EDGE = 8
LANES = 128
LEVELS = 3
STEP_PRIMAL = 0.5
STEP_DUAL = 0.5
F32 = jnp.float32
BF16 = jnp.bfloat16
VMEM = pl.BlockSpec(memory_space=pltpu.VMEM)
SMEM = pl.BlockSpec(memory_space=pltpu.SMEM)


def sincos(angle):
    turn = jnp.floor(angle * (2.0 / math.pi) + 0.5)
    rest = angle - turn * 1.5703125
    rest = rest - turn * 4.83751296997e-04
    rest = rest - turn * 7.54978995489e-08
    square = rest * rest
    sine = rest + rest * square * (
        -1.6666654611e-1 + square * (8.3321608736e-3 - square * 1.9515295891e-4)
    )
    cosine = (1.0 - 0.5 * square) + square * square * (
        4.166664568298827e-2 + square * (-1.388731625493765e-3 + square * 2.443315711809948e-5)
    )
    odd = jnp.abs(turn) == 1.0
    far = jnp.abs(turn) == 2.0
    sin_out = jnp.where(odd, turn * cosine, jnp.where(far, -sine, sine))
    cos_out = jnp.where(odd, -turn * sine, jnp.where(far, -cosine, cosine))
    return sin_out, cos_out


def root_of_unity(number, count):
    number = lax.rem(number, jnp.int32(count))
    number = jnp.where(number >= count // 2, number - count, number)
    return sincos(number.astype(F32) * (2.0 * math.pi / count))


def halves(value):
    high = value.astype(BF16)
    return high, (value - high.astype(F32)).astype(BF16)


def dot(left, right, transposed=False):
    dims = (((1,), (1 if transposed else 0,)), ((), ()))
    return lax.dot_general(left, right, dims, preferred_element_type=F32)


def dot_three(left, right_high, right_low, transposed=False):
    rows = left.shape[0]
    high, low = halves(left)
    both = dot(jnp.concatenate([high, low], axis=0), right_high, transposed)
    return both[:rows] + both[rows:] + dot(high, right_low, transposed)


def prepare_body(phase, weight, rows_col, rows_lane, cos_ref, sin_ref, g_high, g_low, r_ref, rt_ref, slabs):
    full_rows, full_cols = phase.shape
    vis = weight.shape[1]
    picked = rows_col.shape[0]
    step = 16

    def screen(i, carry):
        at = pl.ds(pl.multiple_of(i * step, step), step)
        sine, cosine = sincos(phase[at, :])
        cos_ref[at, :] = cosine
        sin_ref[at, :] = sine
        return carry

    lax.fori_loop(0, full_rows // step, screen, 0)

    sine, cosine = root_of_unity(
        rows_col[:, 0:1] * lax.broadcasted_iota(jnp.int32, (picked, full_rows), 1), full_rows
    )
    scale = 1.0 / math.sqrt(full_rows)
    high, low = halves(jnp.concatenate([cosine * scale, -sine * scale], axis=0))
    r_ref[...] = jnp.concatenate([high, low], axis=0)
    sine, cosine = root_of_unity(
        rows_lane[0:1, :] * lax.broadcasted_iota(jnp.int32, (full_rows, picked), 0), full_rows
    )
    high, low = halves(jnp.concatenate([cosine * scale, -sine * scale], axis=1))
    rt_ref[...] = jnp.concatenate([high, high, low], axis=1)

    half = full_cols // 2
    scale = 1.0 / math.sqrt(full_cols)
    count = vis // LANES
    for k in range(count):
        slabs[k] = weight[:, k * LANES : (k + 1) * LANES] * scale
    even_high, even_low = halves(
        jnp.concatenate([slabs[k, pl.ds(0, half, 2), :] for k in range(count)], axis=1)
    )
    odd_high, odd_low = halves(
        jnp.concatenate([slabs[k, pl.ds(1, half, 2), :] for k in range(count)], axis=1)
    )
    tile = 64

    def transform(i, carry):
        base = pl.multiple_of(i * tile, tile)
        line = base + lax.broadcasted_iota(jnp.int32, (tile, half), 0)
        cell = 2 * lax.broadcasted_iota(jnp.int32, (tile, half), 1)
        sine, cosine = root_of_unity(line * cell, full_cols)
        even = dot_three(jnp.concatenate([cosine, -sine], axis=0), even_high, even_low)
        sine, cosine = root_of_unity(line * (cell + 1), full_cols)
        odd = dot_three(jnp.concatenate([cosine, -sine], axis=0), odd_high, odd_low)
        for where, total in ((base, even + odd), (base + half, even - odd)):
            where = pl.multiple_of(where, tile)
            high, low = halves(jnp.concatenate([total[:tile], total[tile:]], axis=1))
            g_high[pl.ds(where, tile), :] = high
            g_low[pl.ds(where, tile), :] = low
        return carry

    lax.fori_loop(0, half // tile, transform, 0)


def forward_body(image, cos_ref, sin_ref, g_high, g_low, r_ref, data, total):
    full_rows, full_cols = cos_ref.shape
    picked = r_ref.shape[0] // 4
    vis = g_high.shape[1] // 2
    chunk = 256
    total[...] = jnp.zeros_like(total)
    stacked = r_ref[...]
    high_rows = r_ref[0 : 2 * picked, :]

    def add(i, carry):
        at = pl.ds(pl.multiple_of(i * chunk, chunk), chunk)
        block = image[:, at]

        def rows_of(screen):
            high, low = halves(block * screen[:, at])
            both = dot(stacked, high)
            return both[: 2 * picked] + both[2 * picked :] + dot(high_rows, low)

        real = rows_of(cos_ref)
        imag = rows_of(sin_ref)
        spectrum = jnp.concatenate(
            [real[:picked] - imag[picked:], imag[:picked] + real[picked:]], axis=0
        )
        total[...] += dot_three(spectrum, g_high[at, :], g_low[at, :])
        return carry

    lax.fori_loop(0, full_cols // chunk, add, 0)
    sums = total[...]
    real = sums[:picked, :vis] - sums[picked:, vis:] - data[0]
    imag = sums[:picked, vis:] + sums[picked:, :vis] - data[1]
    total[...] = jnp.concatenate(
        [jnp.concatenate([real, imag], axis=1), jnp.concatenate([imag, -real], axis=1)], axis=0
    )


def backward_chunk(misfit, at, cos_ref, sin_ref, g_high, g_low, rt_ref):
    picked = misfit.shape[0] // 2
    back = dot_three(misfit, g_high[at, :], g_low[at, :], True)
    swapped = jnp.concatenate([back[picked:], -back[:picked]], axis=0)
    high, low = halves(jnp.concatenate([back, swapped], axis=1))
    grid = dot(rt_ref[...], jnp.concatenate([high, low, high], axis=0))
    chunk = back.shape[1]
    return cos_ref[:, at] * grid[:, :chunk] + sin_ref[:, at] * grid[:, chunk:]


def measure_body(image, cos_ref, sin_ref, g_high, g_low, r_ref, rt_ref, data, out, total):
    forward_body(image, cos_ref, sin_ref, g_high, g_low, r_ref, data, total)
    chunk = 256

    def back(i, carry):
        at = pl.ds(pl.multiple_of(i * chunk, chunk), chunk)
        out[:, at] = backward_chunk(total[...], at, cos_ref, sin_ref, g_high, g_low, rt_ref)
        return carry

    lax.fori_loop(0, out.shape[1] // chunk, back, 0)


def lane_index(width):
    return lax.broadcasted_iota(jnp.int32, (1, width), 1)


def turned(value, distance):
    distance = distance % value.shape[-1]
    return value if distance == 0 else pltpu.roll(value, distance, value.ndim - 1)


def synthesis_body(dual, taps, levels, out, spill_right, spill_left, padded, plus, minus):
    bases, channels, rows, cols = dual.shape
    tall = rows + 2 * EDGE
    out[...] = jnp.zeros_like(out)
    plus[...] = jnp.zeros_like(plus)
    minus[...] = jnp.zeros_like(minus)
    padded[:, : 2 * EDGE, :] = jnp.zeros((channels, 2 * EDGE, cols), F32)
    padded[:, rows + 2 * EDGE :, :] = jnp.zeros((channels, 2 * EDGE, cols), F32)

    def one(q, carry):
        padded[:, 2 * EDGE : 2 * EDGE + rows, :] = dual[q]
        for level in range(LEVELS):

            @pl.when(levels[q] == level + 1)
            def _():
                gap = 2**level
                for c in range(channels):
                    mixed = taps[6 * q + 1] * padded[c, EDGE : EDGE + tall, :]
                    mixed += taps[6 * q] * padded[c, EDGE + gap : EDGE + gap + tall, :]
                    mixed += taps[6 * q + 2] * padded[c, EDGE - gap : EDGE - gap + tall, :]
                    out[c] += taps[6 * q + 4] * mixed
                    minus[level, c] += taps[6 * q + 3] * mixed
                    plus[level, c] += taps[6 * q + 5] * mixed

        return carry

    lax.fori_loop(0, bases, one, 0)
    lane = lane_index(cols)
    near = lane_index(LANES)
    right = jnp.zeros((tall, LANES), F32)
    left = jnp.zeros((tall, LANES), F32)
    for c in range(channels):
        total = out[c]
        to_right = jnp.zeros((tall, LANES), F32)
        to_left = jnp.zeros((tall, LANES), F32)
        for level in range(LEVELS):
            gap = 2**level
            moved = turned(plus[level, c], gap)
            total += jnp.where(lane >= gap, moved, 0.0)
            to_right += jnp.where(near < gap, moved[:, :LANES], 0.0)
            moved = turned(minus[level, c], -gap)
            total += jnp.where(lane < cols - gap, moved, 0.0)
            to_left += jnp.where(near >= LANES - gap, moved[:, cols - LANES :], 0.0)
        out[c] = total
        right += turned(to_right, HALO * c)
        left += turned(to_left, -HALO * c)
    spill_right[...] = right
    spill_left[...] = left


def widen(tile, cols, at_end):
    if cols == LANES:
        return tile
    rest = jnp.zeros((tile.shape[0], cols - LANES), F32)
    return jnp.concatenate([rest, tile] if at_end else [tile, rest], axis=1)


def update_body(
    now, gradient, synth, side_low, side_high, top, bottom, updated, leading, pack_left, pack_right
):
    channels, rows, cols = now.shape
    near = lane_index(LANES)
    to_left = jnp.zeros((rows, LANES), F32)
    to_right = jnp.zeros((rows, LANES), F32)
    none = jnp.zeros((rows - EDGE, cols), F32)

    def folded(side):
        inside = side[EDGE : EDGE + rows, :]
        rest = jnp.zeros((rows - EDGE, LANES), F32)
        inside += jnp.concatenate([side[:EDGE, :], rest], axis=0)
        inside += jnp.concatenate([rest, side[EDGE + rows :, :]], axis=0)
        return inside

    low = folded(side_low)
    high = folded(side_high)
    for c in range(channels):
        total = synth[c, EDGE : EDGE + rows, :]
        total += jnp.concatenate([top[c], none], axis=0)
        total += jnp.concatenate([none, bottom[c]], axis=0)
        total += widen(jnp.where(near < HALO, turned(low, -HALO * c), 0.0), cols, False)
        total += widen(jnp.where(near >= LANES - HALO, turned(high, HALO * c), 0.0), cols, True)
        before = now[c]
        after = jnp.maximum(before - STEP_PRIMAL * (gradient[c] + total), 0.0)
        updated[c] = after
        ahead = 2.0 * after - before
        leading[c] = ahead
        to_left += turned(jnp.where(near < HALO, ahead[:, :LANES], 0.0), HALO * c)
        to_right += turned(
            jnp.where(near >= LANES - HALO, ahead[:, cols - LANES :], 0.0), -HALO * c
        )
    pack_left[...] = to_left
    pack_right[...] = to_right


def analysis_body(
    leading, side_low, side_high, top, bottom, dual, taps, levels, radius, out, fields, mixed
):
    bases, channels, rows, cols = dual.shape
    near = lane_index(LANES)
    for c in range(channels):
        field = jnp.concatenate([top[c], leading[c], bottom[c]], axis=0)
        before = turned(side_low[...], HALO * c)
        behind = turned(side_high[...], -HALO * c)
        fields[0, c] = field
        for level in range(LEVELS):
            gap = 2**level
            moved = turned(field, gap)
            first = jnp.where(near < gap, turned(before, gap), moved[:, :LANES])
            if cols > LANES:
                first = jnp.concatenate([first, moved[:, LANES:]], axis=1)
            fields[1 + 2 * level, c] = first
            moved = turned(field, -gap)
            last = jnp.where(near >= LANES - gap, turned(behind, -gap), moved[:, cols - LANES :])
            if cols > LANES:
                last = jnp.concatenate([moved[:, : cols - LANES], last], axis=1)
            fields[2 + 2 * level, c] = last

    def one(q, carry):
        for level in range(LEVELS):

            @pl.when(levels[q] == level + 1)
            def _():
                gap = 2**level
                for c in range(channels):
                    mixed[c] = (
                        taps[6 * q + 3] * fields[1 + 2 * level, c]
                        + taps[6 * q + 4] * fields[0, c]
                        + taps[6 * q + 5] * fields[2 + 2 * level, c]
                    )
                for c in range(channels):
                    value = taps[6 * q] * mixed[c, EDGE - gap : EDGE - gap + rows, :]
                    value += taps[6 * q + 1] * mixed[c, EDGE : EDGE + rows, :]
                    value += taps[6 * q + 2] * mixed[c, EDGE + gap : EDGE + gap + rows, :]
                    out[q, c] = dual[q, c] + STEP_DUAL * value

        energy = out[q, 0] * out[q, 0]
        for c in range(1, channels):
            energy += out[q, c] * out[q, c]
        factor = radius[q] / jnp.maximum(jnp.sqrt(energy), radius[q])
        for c in range(channels):
            out[q, c] = out[q, c] * factor
        return carry

    lax.fori_loop(0, bases, one, 0)


def local_call(body, shapes, in_specs, scratch, name):
    return pl.pallas_call(
        body,
        out_shape=shapes,
        in_specs=in_specs,
        out_specs=jax.tree.map(lambda _: VMEM, shapes),
        scratch_shapes=scratch,
        compiler_params=pltpu.CompilerParams(vmem_limit_bytes=58 * 1024 * 1024),
        name=name,
    )


def arr(*shape, dtype=F32):
    return jax.ShapeDtypeStruct(shape, dtype)


def neighbour(value, across, along):
    nc, nt = lax.axis_size("chan"), lax.axis_size("tblk")
    route = [
        (c * nt + t, (c + across) * nt + t + along)
        for c in range(nc)
        for t in range(nt)
        if 0 <= c + across < nc and 0 <= t + along < nt
    ]
    return lax.ppermute(value, ("chan", "tblk"), route)


def sides(pack_a, pack_b, rows):
    low = jnp.concatenate(
        [
            neighbour(pack_a[2], 1, 1),
            neighbour(pack_a[1], 1, 0),
            neighbour(pack_a[0], 1, -1),
        ],
        axis=0,
    )
    high = jnp.concatenate(
        [
            neighbour(pack_b[2], -1, 1),
            neighbour(pack_b[1], -1, 0),
            neighbour(pack_b[0], -1, -1),
        ],
        axis=0,
    )
    return low, high


def per_device(sky, dual, phase, rows_at, weight, vis_data, filters, level_counts, radius):
    channels, rows, cols = sky.shape
    bases = dual.shape[0]
    full_rows, full_cols = phase.shape[2:]
    vis = weight.shape[3]
    picked = rows_at.shape[2]
    tall = rows + 2 * EDGE
    taps = filters.reshape(-1)
    data = vis_data[0, 0]
    image_shape = arr(full_rows, full_cols)
    cos_s, sin_s, g_high, g_low, r_mat, rt_mat = local_call(
        prepare_body,
        (
            image_shape,
            image_shape,
            arr(full_cols, 2 * vis, dtype=BF16),
            arr(full_cols, 2 * vis, dtype=BF16),
            arr(4 * picked, full_rows, dtype=BF16),
            arr(full_rows, 6 * picked, dtype=BF16),
        ),
        [VMEM] * 4,
        [pltpu.VMEM((vis // LANES, full_cols, LANES), F32)],
        "prepare",
    )(phase[0, 0], weight[0, 0], rows_at[0, 0][:, None], rows_at[0, 0][None, :])
    for _ in range(ITERS):
        spread = lax.all_to_all(sky, "chan", split_axis=0, concat_axis=2, tiled=True)
        whole = lax.all_gather(spread[0], "tblk", axis=0, tiled=True)
        synth, spill_right, spill_left = local_call(
            synthesis_body,
            (arr(channels, tall, cols), arr(tall, LANES), arr(tall, LANES)),
            [VMEM, SMEM, SMEM],
            [
                pltpu.VMEM((channels, rows + 4 * EDGE, cols), F32),
                pltpu.VMEM((LEVELS, channels, tall, cols), F32),
                pltpu.VMEM((LEVELS, channels, tall, cols), F32),
            ],
            "synthesis",
        )(dual, taps, level_counts)
        cut = lambda spill: (spill[:EDGE], spill[EDGE : EDGE + rows], spill[EDGE + rows :])
        low, high = sides(cut(spill_right), cut(spill_left), rows)
        low = jnp.concatenate([low[:EDGE], low[EDGE : EDGE + rows], low[EDGE + rows :]], axis=0)
        top = neighbour(synth[:, EDGE + rows :], 0, 1)
        bottom = neighbour(synth[:, :EDGE], 0, -1)
        part = local_call(
            measure_body,
            image_shape,
            [VMEM] * 8,
            [pltpu.VMEM((2 * picked, 2 * vis), F32)],
            "measure",
        )(whole, cos_s, sin_s, g_high, g_low, r_mat, rt_mat, data)
        summed = lax.psum_scatter(part, "tblk", scatter_dimension=0, tiled=True)
        gradient = lax.all_to_all(summed[None], "chan", split_axis=2, concat_axis=0, tiled=True)
        updated, leading, pack_left, pack_right = local_call(
            update_body,
            (sky_shape := arr(channels, rows, cols), sky_shape, arr(rows, LANES), arr(rows, LANES)),
            [VMEM] * 7,
            [],
            "update",
        )(sky, gradient, synth, low, high, top, bottom)
        edges = lambda pack: (pack[:EDGE], pack, pack[rows - EDGE :])
        low, high = sides(edges(pack_right), edges(pack_left), rows)
        top = neighbour(leading[:, rows - EDGE :], 0, 1)
        bottom = neighbour(leading[:, :EDGE], 0, -1)
        dual = local_call(
            analysis_body,
            arr(*dual.shape),
            [VMEM] * 6 + [SMEM] * 3,
            [
                pltpu.VMEM((1 + 2 * LEVELS, channels, tall, cols), F32),
                pltpu.VMEM((channels, tall, cols), F32),
            ],
            "analysis",
        )(leading, low, high, top, bottom, dual, taps, level_counts, radius)
        sky = updated
    return sky, dual


def solution(mesh):
    placed = (
        P(None, "tblk", "chan"),
        P(None, None, "tblk", "chan"),
        P("chan", "tblk", None, None),
        P("chan", "tblk", None),
        P("chan", "tblk", None, None),
        P("chan", "tblk", None, None, None),
        P(),
        P(),
        P(),
    )
    return jax.shard_map(
        per_device,
        mesh=mesh,
        in_specs=placed,
        out_specs=(P(None, "tblk", "chan"), P(None, None, "tblk", "chan")),
        check_vma=False,
    )
```

time: 822 us -> 314 us (0.38); the launches traced: 811 us -> 311 us
  matrix products: 351 us -> 0 us
  other arithmetic: 199 us -> 11.7 us
  Pallas kernels: 0 us -> 66.4 us
  local copies, waits for them, and re-layouts: 72.9 us -> 26.2 us
  starting transfers between devices: 61.1 us -> 105 us
  between operations: 55.8 us -> 14.2 us
  blocking collectives: 11.1 us -> 22.4 us
    dot_general x40 -> x0, matrix products: 351 us -> none  [product(): jnp.einsum(form, left, right, precision=FULL_PRECISION, preferred_element...]
    add x24 -> x0, other arithmetic: 133 us -> none  [the longest x14 55.7 us: filter_back(): across + filter_taps[1, offset + 1] * lax.dynamic_slice_in_dim(padded, fi...]
    pallas_call x0 -> x9, Pallas kernels: none -> 66.4 us  [the longest x2 24.5 us: per_device(): local_call(measure_body, image_shape, [VMEM] * 8, [pltpu.VMEM((2 * picked...]
    ppermute x16 -> x32, starting transfers between devices: 47.5 us -> 96.6 us  [neighbour(): return lax.ppermute(value, ('chan', 'tblk'), route)]
    unnamed x6 -> x4, waiting for transfers between devices: 45.4 us -> 0.07 us
    all_gather x2, waiting for transfers between devices: 0.01 us -> 43.4 us  [per_device(): whole = lax.all_gather(spread[0], 'tblk', axis=0, tiled=True)]
    unnamed x18 -> x2, other arithmetic: 43.9 us -> 3.95 us
    reduce_scatter x0 -> x2, waiting for transfers between devices: none -> 16 us  [per_device(): summed = lax.psum_scatter(part, 'tblk', scatter_dimension=0, tiled=True)]
  transfers between devices with their start and end apart: 23 -> 38, of which waited for: 8 -> 5; matrix products, arithmetic and copies ran while one was open for 24% -> 10% of each run, Pallas kernels for 0% -> 10%
where the time goes in v1:
time: 314 us; the launch traced here: 311 us
  starting transfers between devices  105 us (33%)
  Pallas kernels  66.4 us (21%)
  waiting for transfers between devices  65.5 us (21%)
  local copies, waits for them, and re-layouts  26.2 us (8%)
  blocking collectives  22.4 us (7%)
  between operations  14.2 us (5%)
  other arithmetic  11.7 us (4%)
    ppermute x32, starting transfers between devices, neighbour(): return lax.ppermute(value, ('chan', 'tblk'), route)  96.6 us
    all_gather x2, waiting for transfers between devices, per_device(): whole = lax.all_gather(spread[0], 'tblk', axis=0, tiled=True)  43.4 us
    pallas_call x2, Pallas kernels, per_device(): local_call(measure_body, image_shape, [VMEM] * 8, [pltpu.VMEM((2 * picked...  24.5 us
    all_to_all x2, blocking collectives, per_device(): lax.all_to_all(sky, 'chan', split_axis=0, concat_axis=2, tiled=True)  22.4 us
    reduce_scatter x2, waiting for transfers between devices, per_device(): summed = lax.psum_scatter(part, 'tblk', scatter_dimension=0, tiled=True)  16 us
    pallas_call x1, Pallas kernels, per_device(): local_call(prepare_body, (image_shape, image_shape, arr(full_cols, 2 * vi...  14.1 us
    pallas_call x2, Pallas kernels, per_device(): local_call(analysis_body, arr(*dual.shape), [VMEM] * 6 + [SMEM] * 3, [plt...  13 us
    pallas_call x2, Pallas kernels, per_device(): local_call(synthesis_body, (arr(channels, tall, cols), arr(tall, LANES),...  10.4 us
  transfers between devices with their start and end apart: 38, of which 5 were waited for; matrix products, arithmetic and copies ran while one was open for 10% of the time, Pallas kernels for 10%

profile of v1, /device:TPU:11, one launch (start us, length us, event | category | flops | bytes accessed | tf_op | source)
XLA Modules:
  0.0 311.2 jit_solution(921405604134201199)
XLA Ops:
  7.2 10.8 %all_to_all.66 = f32[4,64,256]{2,1,0:T(8,128)S(1)} all-to-all(f32[4,64,256]{2,1,0:T(8,128)} %now.1), channel_id=1, replica_groups=mesh['chan'=4,'tblk'=8] {'chan'}, dimensions={0} | all-to-all | bytes 524288 | tf_op jit(solution)/shard_map/all_to_all | solution.py:408
  19.0 1.4 copy.22.rows_col
  20.4 14.1 %prepare.1 = (f32[512,1024]{1,0:T(8,128)}, f32[512,1024]{1,0:T(8,128)}, bf16[1024,512]{1,0:T(8,128)(2,1)}, bf16[1024,512]{1,0:T(8,128)(2,1)}, bf16[256,512]{1,0:T(8,128)(2,1)}, /*index=5*/bf16[512,384]{1,0:T(8,128)(2,1)}) custom-call(f32[512,1024]{1,0:T(8,128)} %bitcast.33, f32[1024,256]{1,0:T(8,128)} %bitcast.36, s32[64,1]{1,0:T(8,128)} %copy.22.rows_col, ...), custom_call_target="tpu_custom_call" | custom-call | tf_op jit(solution)/shard_map/prepare/pallas_call | solution.py:393
  34.5 14.8 %all-gather.3.cloned.1.call-done.image = f32[512,1024]{1,0:T(8,128)} async-done(((f32[64,1024]{1,0:T(8,128)}), f32[512,1024]{1,0:T(8,128)}) %all-gather.3.cloned.1.call-update) | async-done | bytes 2097168 | tf_op jit(solution)/shard_map/all_gather | solution.py:409
  49.3 12.3 %measure.2 = f32[512,1024]{1,0:T(8,128)} custom-call(f32[512,1024]{1,0:T(8,128)} %all-gather.3.cloned.1.call-done.image, f32[512,1024]{1,0:T(8,128)} %get-tuple-element.22.cos_ref, f32[512,1024]{1,0:T(8,128)} %get-tuple-element.23.sin_ref, bf16[1024,512]{1,0:T(8,128)(2,1)} %get-tuple-element.24.g_high, bf16[1024,512]{1,0:T(8,128)(2,1)} %get-tuple-element.25.g_low, ...), custom_call_target="tpu_custom_call" | custom-call | tf_op jit(solution)/shard_map/measure/pallas_call | solution.py:426
  63.0 5.2 %synthesis.2 = (f32[4,80,256]{2,1,0:T(8,128)}, f32[80,128]{1,0:T(8,128)}, f32[80,128]{1,0:T(8,128)}) custom-call(f32[9,4,64,256]{3,2,1,0:T(8,128)} %dual.3, f32[54]{0:T(128)} %reshape.9.taps, s32[9]{0:T(128)} %levels.7), custom_call_target="tpu_custom_call" | custom-call | tf_op jit(solution)/shard_map/synthesis/pallas_call | solution.py:410
  68.9 3.3 %collective-permute-start.2 = (f32[8,128]{1,0:T(8,128)S(1)}, f32[8,128]{1,0:T(8,128)S(1)}, u32[]{:S(2)}, u32[]{:S(2)}) collective-permute-start(f32[8,128]{1,0:T(8,128)S(1)} %get-tuple-element.57), channel_id=1, source_target_pairs={{1,8},{2,9},{3,10},{4,11},{5,12},{6,13},{7,14},{9,16},{10,17},{11,... | collective-permute-start | bytes 12296 | tf_op jit(solution)/shard_map/ppermute | solution.py:360
  72.9 3.1 collective-permute-start.1
  76.0 3.8 %collective-permute-start = (f32[8,128]{1,0:T(8,128)S(1)}, f32[8,128]{1,0:T(8,128)S(1)}, u32[]{:S(2)}, u32[]{:S(2)}) collective-permute-start(f32[8,128]{1,0:T(8,128)S(1)} %get-tuple-element.56), channel_id=1, source_target_pairs={{0,9},{1,10},{2,11},{3,12},{4,13},{5,14},{6,15},{8,17},{9,18},{10,... | collective-permute-start | bytes 12296 | tf_op jit(solution)/shard_map/ppermute | solution.py:360
  80.6 1.9 collective-permute-start.5
  83.3 3.0 collective-permute-start.4
  86.3 16.0 %reduce-scatter.3.cloned.1.call-done = f32[64,1024]{1,0:T(8,128)} async-done(((f32[512,1024]{1,0:T(8,128)}), f32[64,1024]{1,0:T(8,128)}) %reduce-scatter.3.cloned.1.call-update) | async-done | bytes 262160 | tf_op jit(solution)/shard_map/reduce_scatter | solution.py:433
  102.3 1.2 copy.23
  104.0 2.0 reduce
  106.0 1.0 reshape.10
  107.0 4.6 %all-to-all-start.1 = ((f32[4,1,16384]{2,1,0:T(1,128)}), f32[4,1,16384]{2,1,0:T(1,128)S(1)}, u32[]{:S(2)}, u32[]{:S(2)}) async-start(f32[4,1,16384]{2,1,0:T(1,128)} %reshape.10), calls=%async_computation.2 | async-start | bytes 524288 | tf_op jit(solution)/shard_map/all_to_all | solution.py:434
  112.4 3.8 %collective-permute-start.3 = (f32[8,128]{1,0:T(8,128)S(1)}, f32[8,128]{1,0:T(8,128)S(1)}, u32[]{:S(2)}, u32[]{:S(2)}) collective-permute-start(f32[8,128]{1,0:T(8,128)S(1)} %get-tuple-element.54), channel_id=1, source_target_pairs={{8,1},{9,2},{10,3},{11,4},{12,5},{13,6},{14,7},{16,9},{17,10},{18,... | collective-permute-start | bytes 12296 | tf_op jit(solution)/shard_map/ppermute | solution.py:360
  116.2 2.5 collective-permute-start.6
  118.7 1.9 collective-permute-start.7
  121.9 1.4 reduce.1
  123.9 0.9 copy.25
  125.5 2.2 update.2
  127.6 11.6 %all_to_all.67 = f32[4,64,256]{2,1,0:T(8,128)S(1)} all-to-all(f32[4,64,256]{2,1,0:T(8,128)} %get-tuple-element.31.now), channel_id=1, replica_groups=mesh['chan'=4,'tblk'=8] {'chan'}, dimensions={0} | all-to-all | bytes 524288 | tf_op jit(solution)/shard_map/all_to_all | solution.py:408
  140.3 28.7 %all-gather.5.cloned.1.call-done.image = f32[512,1024]{1,0:T(8,128)} async-done(((f32[64,1024]{1,0:T(8,128)}), f32[512,1024]{1,0:T(8,128)}) %all-gather.5.cloned.1.call-update) | async-done | bytes 2097168 | tf_op jit(solution)/shard_map/all_gather | solution.py:409
  168.9 12.2 %measure.3 = f32[512,1024]{1,0:T(8,128)} custom-call(f32[512,1024]{1,0:T(8,128)} %all-gather.5.cloned.1.call-done.image, f32[512,1024]{1,0:T(8,128)} %get-tuple-element.22.cos_ref, f32[512,1024]{1,0:T(8,128)} %get-tuple-element.23.sin_ref, bf16[1024,512]{1,0:T(8,128)(2,1)} %get-tuple-element.24.g_high, bf16[1024,512]{1,0:T(8,128)(2,1)} %get-tuple-element.25.g_low, ...), custom_call_target="tpu_custom_call" | custom-call | tf_op jit(solution)/shard_map/measure/pallas_call | solution.py:426
  181.9 3.1 collective-permute-start.9
  185.1 3.6 %collective-permute-start.10 = (f32[8,128]{1,0:T(8,128)S(1)}, f32[8,128]{1,0:T(8,128)S(1)}, u32[]{:S(2)}, u32[]{:S(2)}) collective-permute-start(f32[8,128]{1,0:T(8,128)S(1)} %get-tuple-element.65), channel_id=1, source_target_pairs={{1,8},{2,9},{3,10},{4,11},{5,12},{6,13},{7,14},{9,16},{10,17},{11,... | collective-permute-start | bytes 12296 | tf_op jit(solution)/shard_map/ppermute | solution.py:360
  188.6 2.9 collective-permute-start.8
  191.6 4.0 %collective-permute-start.12 = (f32[64,128]{1,0:T(8,128)S(1)}, f32[64,128]{1,0:T(8,128)S(1)}, u32[]{:S(2)}, u32[]{:S(2)}) collective-permute-start(f32[64,128]{1,0:T(8,128)S(1)} %copy-done.9), channel_id=1, source_target_pairs={{8,0},{9,1},{10,2},{11,3},{12,4},{13,5},{14,6},{15,7},{16,8},{17,9... | collective-permute-start | bytes 98312 | tf_op jit(solution)/shard_map/ppermute | solution.py:360
  195.6 1.9 collective-permute-start.13
  197.5 0.8 fusion.3
  198.3 1.9 collective-permute-start.11
  200.2 3.6 %collective-permute-start.14 = (f32[4,8,256]{2,1,0:T(8,128)S(1)}, f32[4,8,256]{2,1,0:T(8,128)S(1)}, u32[]{:S(2)}, u32[]{:S(2)}) collective-permute-start(f32[4,8,256]{2,1,0:T(8,128)S(1)} %get-tuple-element.49), channel_id=1, source_target_pairs={{0,1},{1,2},{2,3},{3,4},{4,5},{5,6},{6,7},{8,9},{9,10},{10,11},{11... | collective-permute-start | bytes 98312 | tf_op jit(solution)/shard_map/ppermute | solution.py:360
  203.9 2.1 collective-permute-start.15
  207.3 3.0 collective-permute-done.15.bottom
  210.9 6.5 %analysis.2.dual = f32[9,4,64,256]{3,2,1,0:T(8,128)} custom-call(f32[4,64,256]{2,1,0:T(8,128)} %get-tuple-element.32.leading, f32[80,128]{1,0:T(8,128)} %pad_maximum_fusion.2.side_low, f32[80,128]{1,0:T(8,128)} %pad_maximum_fusion.3.side_high, f32[4,8,256]{2,1,0:T(8,128)} %copy-done.1, f32[4,8,256]{2,1,0:T(8,128)} %copy-done.3, f32[9,4,64,256]{3,2,1,0:T(8,128)} %dual.3, ...), custom_call_target="tpu_custom_call" | custom-call | tf_op jit(solution)/shard_map/analysis/pallas_call | solution.py:446
  217.4 5.2 %synthesis.3 = (f32[4,80,256]{2,1,0:T(8,128)}, f32[80,128]{1,0:T(8,128)}, f32[80,128]{1,0:T(8,128)}) custom-call(f32[9,4,64,256]{3,2,1,0:T(8,128)} %analysis.2.dual, f32[54]{0:T(128)} %reshape.9.taps, s32[9]{0:T(128)} %levels.7), custom_call_target="tpu_custom_call" | custom-call | tf_op jit(solution)/shard_map/synthesis/pallas_call | solution.py:410
  224.1 1.9 collective-permute-start.18
  226.0 3.8 %collective-permute-start.17 = (f32[64,128]{1,0:T(8,128)S(1)}, f32[64,128]{1,0:T(8,128)S(1)}, u32[]{:S(2)}, u32[]{:S(2)}) collective-permute-start(f32[64,128]{1,0:T(8,128)S(1)} %slice.99), channel_id=1, source_target_pairs={{0,8},{1,9},{2,10},{3,11},{4,12},{5,13},{6,14},{7,15},{8,16},{9,17... | collective-permute-start | bytes 98312 | tf_op jit(solution)/shard_map/ppermute | solution.py:360
  229.7 5.2 %collective-permute-start.16 = (f32[8,128]{1,0:T(8,128)S(1)}, f32[8,128]{1,0:T(8,128)S(1)}, u32[]{:S(2)}, u32[]{:S(2)}) collective-permute-start(f32[8,128]{1,0:T(8,128)S(1)} %get-tuple-element.52), channel_id=1, source_target_pairs={{0,9},{1,10},{2,11},{3,12},{4,13},{5,14},{6,15},{8,17},{9,18},{10,... | collective-permute-start | bytes 12296 | tf_op jit(solution)/shard_map/ppermute | solution.py:360
  236.4 1.9 collective-permute-start.21
  238.3 3.0 collective-permute-start.20
  241.3 1.2 copy.28
  242.5 2.0 reduce.2
  244.5 1.0 reshape.12
  245.5 3.4 %all-to-all-start.3 = ((f32[4,1,16384]{2,1,0:T(1,128)}), f32[4,1,16384]{2,1,0:T(1,128)S(1)}, u32[]{:S(2)}, u32[]{:S(2)}) async-start(f32[4,1,16384]{2,1,0:T(1,128)} %reshape.12), calls=%async_computation.5 | async-start | bytes 524288 | tf_op jit(solution)/shard_map/all_to_all | solution.py:434
  248.9 0.8 fusion
  249.7 5.7 %collective-permute-start.19 = (f32[8,128]{1,0:T(8,128)S(1)}, f32[8,128]{1,0:T(8,128)S(1)}, u32[]{:S(2)}, u32[]{:S(2)}) collective-permute-start(f32[8,128]{1,0:T(8,128)S(1)} %get-tuple-element.50), channel_id=1, source_target_pairs={{8,1},{9,2},{10,3},{11,4},{12,5},{13,6},{14,7},{16,9},{17,10},{18,... | collective-permute-start | bytes 12296 | tf_op jit(solution)/shard_map/ppermute | solution.py:360
  255.4 2.5 collective-permute-start.22
  257.9 1.9 collective-permute-start.23
  261.1 1.4 reduce.3
  263.1 0.9 copy.30
  264.7 2.1 update.3
  267.5 3.6 %collective-permute-start.25 = (f32[64,128]{1,0:T(8,128)}, f32[64,128]{1,0:T(8,128)S(1)}, u32[]{:S(2)}, u32[]{:S(2)}) collective-permute-start(f32[64,128]{1,0:T(8,128)} %get-tuple-element.40), channel_id=1, source_target_pairs={{0,8},{1,9},{2,10},{3,11},{4,12},{5,13},{6,14},{7,15},{8,16},{9,17... | collective-permute-start | bytes 98312 | tf_op jit(solution)/shard_map/ppermute | solution.py:360
  271.7 1.9 collective-permute-start.28
  273.6 3.8 %collective-permute-start.26 = (f32[8,128]{1,0:T(8,128)S(1)}, f32[8,128]{1,0:T(8,128)S(1)}, u32[]{:S(2)}, u32[]{:S(2)}) collective-permute-start(f32[8,128]{1,0:T(8,128)S(1)} %get-tuple-element.61), channel_id=1, source_target_pairs={{1,8},{2,9},{3,10},{4,11},{5,12},{6,13},{7,14},{9,16},{10,17},{11,... | collective-permute-start | bytes 12296 | tf_op jit(solution)/shard_map/ppermute | solution.py:360
  277.5 4.7 %collective-permute-start.24 = (f32[8,128]{1,0:T(8,128)S(1)}, f32[8,128]{1,0:T(8,128)S(1)}, u32[]{:S(2)}, u32[]{:S(2)}) collective-permute-start(f32[8,128]{1,0:T(8,128)S(1)} %get-tuple-element.60), channel_id=1, source_target_pairs={{0,9},{1,10},{2,11},{3,12},{4,13},{5,14},{6,15},{8,17},{9,18},{10,... | collective-permute-start | bytes 12296 | tf_op jit(solution)/shard_map/ppermute | solution.py:360
  282.2 1.9 collective-permute-start.29
  284.1 0.8 fusion.2
  284.9 2.2 collective-permute-start.27
  287.1 4.3 %collective-permute-start.30 = (f32[4,8,256]{2,1,0:T(8,128)S(1)}, f32[4,8,256]{2,1,0:T(8,128)S(1)}, u32[]{:S(2)}, u32[]{:S(2)}) collective-permute-start(f32[4,8,256]{2,1,0:T(8,128)S(1)} %get-tuple-element.47), channel_id=1, source_target_pairs={{0,1},{1,2},{2,3},{3,4},{4,5},{5,6},{6,7},{8,9},{9,10},{10,11},{11... | collective-permute-start | bytes 98312 | tf_op jit(solution)/shard_map/ppermute | solution.py:360
  291.4 1.9 collective-permute-start.31
  294.6 3.0 collective-permute-done.31.bottom
  298.1 6.5 %analysis.3 = f32[9,4,64,256]{3,2,1,0:T(8,128)} custom-call(f32[4,64,256]{2,1,0:T(8,128)} %get-tuple-element.39.leading, f32[80,128]{1,0:T(8,128)} %pad_maximum_fusion.6.side_low, f32[80,128]{1,0:T(8,128)} %pad_maximum_fusion.7.side_high, f32[4,8,256]{2,1,0:T(8,128)} %copy-done, f32[4,8,256]{2,1,0:T(8,128)} %copy-done.2, f32[9,4,64,256]{3,2,1,0:T(8,128)} %analysis.2.dual, ...), custom_call_target="tpu_custom_call" | custom-call | tf_op jit(solution)/shard_map/analysis/pallas_call | solution.py:446
  (93 shorter events, 21.5 us)
Async XLA Ops:
  7.2 42.1 %all-gather.3.cloned.1.call-start = ((), (), s32[]{:S(2)}) async-start(), calls=%async_computation.6 | async-start | bytes 2359296 | tf_op jit(solution)/shard_map/all_gather | solution.py:409
  19.0 83.3 %reduce-scatter.3.cloned.1.call-start = ((), (), s32[]{:S(2)}) async-start(), calls=%async_computation.7 | async-start | bytes 2359296 | tf_op jit(solution)/shard_map/reduce_scatter | solution.py:433
  61.5 0.7 copy-start.8
  68.9 43.5 %collective-permute-start.2 = (f32[8,128]{1,0:T(8,128)S(1)}, f32[8,128]{1,0:T(8,128)S(1)}, u32[]{:S(2)}, u32[]{:S(2)}) collective-permute-start(f32[8,128]{1,0:T(8,128)S(1)} %get-tuple-element.57), channel_id=1, source_target_pairs={{1,8},{2,9},{3,10},{4,11},{5,12},{6,13},{7,14},{9,16},{10,17},{11,... | collective-permute-start | bytes 12296 | tf_op jit(solution)/shard_map/ppermute | solution.py:360
  72.9 45.8 %collective-permute-start.1 = (f32[64,128]{1,0:T(8,128)S(1)}, f32[64,128]{1,0:T(8,128)S(1)}, u32[]{:S(2)}, u32[]{:S(2)}) collective-permute-start(f32[64,128]{1,0:T(8,128)S(1)} %slice.85), channel_id=1, source_target_pairs={{0,8},{1,9},{2,10},{3,11},{4,12},{5,13},{6,14},{7,15},{8,16},{9,17... | collective-permute-start | bytes 98312 | tf_op jit(solution)/shard_map/ppermute | solution.py:360
  76.0 40.2 %collective-permute-start = (f32[8,128]{1,0:T(8,128)S(1)}, f32[8,128]{1,0:T(8,128)S(1)}, u32[]{:S(2)}, u32[]{:S(2)}) collective-permute-start(f32[8,128]{1,0:T(8,128)S(1)} %get-tuple-element.56), channel_id=1, source_target_pairs={{0,9},{1,10},{2,11},{3,12},{4,13},{5,14},{6,15},{8,17},{9,18},{10,... | collective-permute-start | bytes 12296 | tf_op jit(solution)/shard_map/ppermute | solution.py:360
  80.6 40.7 %collective-permute-start.5 = (f32[8,128]{1,0:T(8,128)S(1)}, f32[8,128]{1,0:T(8,128)S(1)}, u32[]{:S(2)}, u32[]{:S(2)}) collective-permute-start(f32[8,128]{1,0:T(8,128)S(1)} %get-tuple-element.55), channel_id=1, source_target_pairs={{9,0},{10,1},{11,2},{12,3},{13,4},{14,5},{15,6},{17,8},{18,9},{19,... | collective-permute-start | bytes 12296 | tf_op jit(solution)/shard_map/ppermute | solution.py:360
  83.3 38.0 %collective-permute-start.4 = (f32[64,128]{1,0:T(8,128)S(1)}, f32[64,128]{1,0:T(8,128)S(1)}, u32[]{:S(2)}, u32[]{:S(2)}) collective-permute-start(f32[64,128]{1,0:T(8,128)S(1)} %slice.88), channel_id=1, source_target_pairs={{8,0},{9,1},{10,2},{11,3},{12,4},{13,5},{14,6},{15,7},{16,8},{17,9... | collective-permute-start | bytes 98312 | tf_op jit(solution)/shard_map/ppermute | solution.py:360
  107.0 14.9 %all-to-all-start.1 = ((f32[4,1,16384]{2,1,0:T(1,128)}), f32[4,1,16384]{2,1,0:T(1,128)S(1)}, u32[]{:S(2)}, u32[]{:S(2)}) async-start(f32[4,1,16384]{2,1,0:T(1,128)} %reshape.10), calls=%async_computation.2 | async-start | bytes 524288 | tf_op jit(solution)/shard_map/all_to_all | solution.py:434
  111.6 57.3 %all-gather.5.cloned.1.call-start = ((), (), s32[]{:S(2)}) async-start(), calls=%async_computation.8 | async-start | bytes 2359296 | tf_op jit(solution)/shard_map/all_gather | solution.py:409
  112.4 8.9 %collective-permute-start.3 = (f32[8,128]{1,0:T(8,128)S(1)}, f32[8,128]{1,0:T(8,128)S(1)}, u32[]{:S(2)}, u32[]{:S(2)}) collective-permute-start(f32[8,128]{1,0:T(8,128)S(1)} %get-tuple-element.54), channel_id=1, source_target_pairs={{8,1},{9,2},{10,3},{11,4},{12,5},{13,6},{14,7},{16,9},{17,10},{18,... | collective-permute-start | bytes 12296 | tf_op jit(solution)/shard_map/ppermute | solution.py:360
  116.2 8.6 %collective-permute-start.6 = (f32[4,8,256]{2,1,0:T(8,128)S(1)}, f32[4,8,256]{2,1,0:T(8,128)S(1)}, u32[]{:S(2)}, u32[]{:S(2)}) collective-permute-start(f32[4,8,256]{2,1,0:T(8,128)S(1)} %get-tuple-element.45), channel_id=1, source_target_pairs={{0,1},{1,2},{2,3},{3,4},{4,5},{5,6},{6,7},{8,9},{9,10},{10,11},{11... | collective-permute-start | bytes 98312 | tf_op jit(solution)/shard_map/ppermute | solution.py:360
  118.7 6.1 %collective-permute-start.7 = (f32[4,8,256]{2,1,0:T(8,128)S(1)}, f32[4,8,256]{2,1,0:T(8,128)S(1)}, u32[]{:S(2)}, u32[]{:S(2)}) collective-permute-start(f32[4,8,256]{2,1,0:T(8,128)S(1)} %get-tuple-element.44), channel_id=1, source_target_pairs={{1,0},{2,1},{3,2},{4,3},{5,4},{6,5},{7,6},{9,8},{10,9},{11,10},{12... | collective-permute-start | bytes 98312 | tf_op jit(solution)/shard_map/ppermute | solution.py:360
  124.8 0.6 copy-start.5
  124.8 0.6 copy-start.7
  140.2 101.1 %reduce-scatter.5.cloned.1.call-start = ((), (), s32[]{:S(2)}) async-start(), calls=%async_computation.9 | async-start | bytes 2359296 | tf_op jit(solution)/shard_map/reduce_scatter | solution.py:433
  181.2 0.8 copy-start.10
  181.2 10.4 %copy-start.9 = (f32[64,128]{1,0:T(8,128)S(1)}, f32[64,128]{1,0:T(8,128)}, u32[]{:S(2)}) copy-start(f32[64,128]{1,0:T(8,128)} %get-tuple-element.34) | copy-start | bytes 98308
  181.9 21.9 %collective-permute-start.9 = (f32[64,128]{1,0:T(8,128)S(1)}, f32[64,128]{1,0:T(8,128)S(1)}, u32[]{:S(2)}, u32[]{:S(2)}) collective-permute-start(f32[64,128]{1,0:T(8,128)S(1)} %copy-done.10), channel_id=1, source_target_pairs={{0,8},{1,9},{2,10},{3,11},{4,12},{5,13},{6,14},{7,15},{8,16},{9,17... | collective-permute-start | bytes 98312 | tf_op jit(solution)/shard_map/ppermute | solution.py:360
  185.1 13.2 %collective-permute-start.10 = (f32[8,128]{1,0:T(8,128)S(1)}, f32[8,128]{1,0:T(8,128)S(1)}, u32[]{:S(2)}, u32[]{:S(2)}) collective-permute-start(f32[8,128]{1,0:T(8,128)S(1)} %get-tuple-element.65), channel_id=1, source_target_pairs={{1,8},{2,9},{3,10},{4,11},{5,12},{6,13},{7,14},{9,16},{10,17},{11,... | collective-permute-start | bytes 12296 | tf_op jit(solution)/shard_map/ppermute | solution.py:360
  188.6 11.6 %collective-permute-start.8 = (f32[8,128]{1,0:T(8,128)S(1)}, f32[8,128]{1,0:T(8,128)S(1)}, u32[]{:S(2)}, u32[]{:S(2)}) collective-permute-start(f32[8,128]{1,0:T(8,128)S(1)} %get-tuple-element.64), channel_id=1, source_target_pairs={{0,9},{1,10},{2,11},{3,12},{4,13},{5,14},{6,15},{8,17},{9,18},{10,... | collective-permute-start | bytes 12296 | tf_op jit(solution)/shard_map/ppermute | solution.py:360
  191.6 15.1 %collective-permute-start.12 = (f32[64,128]{1,0:T(8,128)S(1)}, f32[64,128]{1,0:T(8,128)S(1)}, u32[]{:S(2)}, u32[]{:S(2)}) collective-permute-start(f32[64,128]{1,0:T(8,128)S(1)} %copy-done.9), channel_id=1, source_target_pairs={{8,0},{9,1},{10,2},{11,3},{12,4},{13,5},{14,6},{15,7},{16,8},{17,9... | collective-permute-start | bytes 98312 | tf_op jit(solution)/shard_map/ppermute | solution.py:360
  195.6 11.1 %collective-permute-start.13 = (f32[8,128]{1,0:T(8,128)S(1)}, f32[8,128]{1,0:T(8,128)S(1)}, u32[]{:S(2)}, u32[]{:S(2)}) collective-permute-start(f32[8,128]{1,0:T(8,128)S(1)} %get-tuple-element.63), channel_id=1, source_target_pairs={{9,0},{10,1},{11,2},{12,3},{13,4},{14,5},{15,6},{17,8},{18,9},{19,... | collective-permute-start | bytes 12296 | tf_op jit(solution)/shard_map/ppermute | solution.py:360
  198.3 8.3 %collective-permute-start.11 = (f32[8,128]{1,0:T(8,128)S(1)}, f32[8,128]{1,0:T(8,128)S(1)}, u32[]{:S(2)}, u32[]{:S(2)}) collective-permute-start(f32[8,128]{1,0:T(8,128)S(1)} %get-tuple-element.62), channel_id=1, source_target_pairs={{8,1},{9,2},{10,3},{11,4},{12,5},{13,6},{14,7},{16,9},{17,10},{18,... | collective-permute-start | bytes 12296 | tf_op jit(solution)/shard_map/ppermute | solution.py:360
  200.2 7.0 %collective-permute-start.14 = (f32[4,8,256]{2,1,0:T(8,128)S(1)}, f32[4,8,256]{2,1,0:T(8,128)S(1)}, u32[]{:S(2)}, u32[]{:S(2)}) collective-permute-start(f32[4,8,256]{2,1,0:T(8,128)S(1)} %get-tuple-element.49), channel_id=1, source_target_pairs={{0,1},{1,2},{2,3},{3,4},{4,5},{5,6},{6,7},{8,9},{9,10},{10,11},{11... | collective-permute-start | bytes 98312 | tf_op jit(solution)/shard_map/ppermute | solution.py:360
  203.9 6.4 %collective-permute-start.15 = (f32[4,8,256]{2,1,0:T(8,128)S(1)}, f32[4,8,256]{2,1,0:T(8,128)S(1)}, u32[]{:S(2)}, u32[]{:S(2)}) collective-permute-start(f32[4,8,256]{2,1,0:T(8,128)S(1)} %get-tuple-element.48), channel_id=1, source_target_pairs={{1,0},{2,1},{3,2},{4,3},{5,4},{6,5},{7,6},{9,8},{10,9},{11,10},{12... | collective-permute-start | bytes 98312 | tf_op jit(solution)/shard_map/ppermute | solution.py:360
  207.3 3.0 copy-start.1
  210.3 0.6 copy-start.3
  224.1 25.6 %collective-permute-start.18 = (f32[8,128]{1,0:T(8,128)S(1)}, f32[8,128]{1,0:T(8,128)S(1)}, u32[]{:S(2)}, u32[]{:S(2)}) collective-permute-start(f32[8,128]{1,0:T(8,128)S(1)} %get-tuple-element.53), channel_id=1, source_target_pairs={{1,8},{2,9},{3,10},{4,11},{5,12},{6,13},{7,14},{9,16},{10,17},{11,... | collective-permute-start | bytes 12296 | tf_op jit(solution)/shard_map/ppermute | solution.py:360
  226.0 31.9 %collective-permute-start.17 = (f32[64,128]{1,0:T(8,128)S(1)}, f32[64,128]{1,0:T(8,128)S(1)}, u32[]{:S(2)}, u32[]{:S(2)}) collective-permute-start(f32[64,128]{1,0:T(8,128)S(1)} %slice.99), channel_id=1, source_target_pairs={{0,8},{1,9},{2,10},{3,11},{4,12},{5,13},{6,14},{7,15},{8,16},{9,17... | collective-permute-start | bytes 98312 | tf_op jit(solution)/shard_map/ppermute | solution.py:360
  229.7 25.7 %collective-permute-start.16 = (f32[8,128]{1,0:T(8,128)S(1)}, f32[8,128]{1,0:T(8,128)S(1)}, u32[]{:S(2)}, u32[]{:S(2)}) collective-permute-start(f32[8,128]{1,0:T(8,128)S(1)} %get-tuple-element.52), channel_id=1, source_target_pairs={{0,9},{1,10},{2,11},{3,12},{4,13},{5,14},{6,15},{8,17},{9,18},{10,... | collective-permute-start | bytes 12296 | tf_op jit(solution)/shard_map/ppermute | solution.py:360
  236.4 24.1 %collective-permute-start.21 = (f32[8,128]{1,0:T(8,128)S(1)}, f32[8,128]{1,0:T(8,128)S(1)}, u32[]{:S(2)}, u32[]{:S(2)}) collective-permute-start(f32[8,128]{1,0:T(8,128)S(1)} %get-tuple-element.51), channel_id=1, source_target_pairs={{9,0},{10,1},{11,2},{12,3},{13,4},{14,5},{15,6},{17,8},{18,9},{19,... | collective-permute-start | bytes 12296 | tf_op jit(solution)/shard_map/ppermute | solution.py:360
  238.3 22.2 %collective-permute-start.20 = (f32[64,128]{1,0:T(8,128)S(1)}, f32[64,128]{1,0:T(8,128)S(1)}, u32[]{:S(2)}, u32[]{:S(2)}) collective-permute-start(f32[64,128]{1,0:T(8,128)S(1)} %slice.102), channel_id=1, source_target_pairs={{8,0},{9,1},{10,2},{11,3},{12,4},{13,5},{14,6},{15,7},{16,8},{17,9... | collective-permute-start | bytes 98312 | tf_op jit(solution)/shard_map/ppermute | solution.py:360
  245.5 15.6 %all-to-all-start.3 = ((f32[4,1,16384]{2,1,0:T(1,128)}), f32[4,1,16384]{2,1,0:T(1,128)S(1)}, u32[]{:S(2)}, u32[]{:S(2)}) async-start(f32[4,1,16384]{2,1,0:T(1,128)} %reshape.12), calls=%async_computation.5 | async-start | bytes 524288 | tf_op jit(solution)/shard_map/all_to_all | solution.py:434
  249.7 10.7 %collective-permute-start.19 = (f32[8,128]{1,0:T(8,128)S(1)}, f32[8,128]{1,0:T(8,128)S(1)}, u32[]{:S(2)}, u32[]{:S(2)}) collective-permute-start(f32[8,128]{1,0:T(8,128)S(1)} %get-tuple-element.50), channel_id=1, source_target_pairs={{8,1},{9,2},{10,3},{11,4},{12,5},{13,6},{14,7},{16,9},{17,10},{18,... | collective-permute-start | bytes 12296 | tf_op jit(solution)/shard_map/ppermute | solution.py:360
  255.4 8.6 %collective-permute-start.22 = (f32[4,8,256]{2,1,0:T(8,128)S(1)}, f32[4,8,256]{2,1,0:T(8,128)S(1)}, u32[]{:S(2)}, u32[]{:S(2)}) collective-permute-start(f32[4,8,256]{2,1,0:T(8,128)S(1)} %get-tuple-element.43), channel_id=1, source_target_pairs={{0,1},{1,2},{2,3},{3,4},{4,5},{5,6},{6,7},{8,9},{9,10},{10,11},{11... | collective-permute-start | bytes 98312 | tf_op jit(solution)/shard_map/ppermute | solution.py:360
  257.9 6.1 %collective-permute-start.23 = (f32[4,8,256]{2,1,0:T(8,128)S(1)}, f32[4,8,256]{2,1,0:T(8,128)S(1)}, u32[]{:S(2)}, u32[]{:S(2)}) collective-permute-start(f32[4,8,256]{2,1,0:T(8,128)S(1)} %get-tuple-element.42), channel_id=1, source_target_pairs={{1,0},{2,1},{3,2},{4,3},{5,4},{6,5},{7,6},{9,8},{10,9},{11,10},{12... | collective-permute-start | bytes 98312 | tf_op jit(solution)/shard_map/ppermute | solution.py:360
  264.0 0.6 copy-start.4
  264.0 0.6 copy-start.6
  267.5 23.9 %collective-permute-start.25 = (f32[64,128]{1,0:T(8,128)}, f32[64,128]{1,0:T(8,128)S(1)}, u32[]{:S(2)}, u32[]{:S(2)}) collective-permute-start(f32[64,128]{1,0:T(8,128)} %get-tuple-element.40), channel_id=1, source_target_pairs={{0,8},{1,9},{2,10},{3,11},{4,12},{5,13},{6,14},{7,15},{8,16},{9,17... | collective-permute-start | bytes 98312 | tf_op jit(solution)/shard_map/ppermute | solution.py:360
  271.7 22.2 %collective-permute-start.28 = (f32[64,128]{1,0:T(8,128)}, f32[64,128]{1,0:T(8,128)S(1)}, u32[]{:S(2)}, u32[]{:S(2)}) collective-permute-start(f32[64,128]{1,0:T(8,128)} %get-tuple-element.41), channel_id=1, source_target_pairs={{8,0},{9,1},{10,2},{11,3},{12,4},{13,5},{14,6},{15,7},{16,8},{17,9... | collective-permute-start | bytes 98312 | tf_op jit(solution)/shard_map/ppermute | solution.py:360
  273.6 11.3 %collective-permute-start.26 = (f32[8,128]{1,0:T(8,128)S(1)}, f32[8,128]{1,0:T(8,128)S(1)}, u32[]{:S(2)}, u32[]{:S(2)}) collective-permute-start(f32[8,128]{1,0:T(8,128)S(1)} %get-tuple-element.61), channel_id=1, source_target_pairs={{1,8},{2,9},{3,10},{4,11},{5,12},{6,13},{7,14},{9,16},{10,17},{11,... | collective-permute-start | bytes 12296 | tf_op jit(solution)/shard_map/ppermute | solution.py:360
  277.5 9.6 %collective-permute-start.24 = (f32[8,128]{1,0:T(8,128)S(1)}, f32[8,128]{1,0:T(8,128)S(1)}, u32[]{:S(2)}, u32[]{:S(2)}) collective-permute-start(f32[8,128]{1,0:T(8,128)S(1)} %get-tuple-element.60), channel_id=1, source_target_pairs={{0,9},{1,10},{2,11},{3,12},{4,13},{5,14},{6,15},{8,17},{9,18},{10,... | collective-permute-start | bytes 12296 | tf_op jit(solution)/shard_map/ppermute | solution.py:360
  282.2 11.8 %collective-permute-start.29 = (f32[8,128]{1,0:T(8,128)S(1)}, f32[8,128]{1,0:T(8,128)S(1)}, u32[]{:S(2)}, u32[]{:S(2)}) collective-permute-start(f32[8,128]{1,0:T(8,128)S(1)} %get-tuple-element.59), channel_id=1, source_target_pairs={{9,0},{10,1},{11,2},{12,3},{13,4},{14,5},{15,6},{17,8},{18,9},{19,... | collective-permute-start | bytes 12296 | tf_op jit(solution)/shard_map/ppermute | solution.py:360
  284.9 9.0 %collective-permute-start.27 = (f32[8,128]{1,0:T(8,128)S(1)}, f32[8,128]{1,0:T(8,128)S(1)}, u32[]{:S(2)}, u32[]{:S(2)}) collective-permute-start(f32[8,128]{1,0:T(8,128)S(1)} %get-tuple-element.58), channel_id=1, source_target_pairs={{8,1},{9,2},{10,3},{11,4},{12,5},{13,6},{14,7},{16,9},{17,10},{18,... | collective-permute-start | bytes 12296 | tf_op jit(solution)/shard_map/ppermute | solution.py:360
  287.1 7.5 %collective-permute-start.30 = (f32[4,8,256]{2,1,0:T(8,128)S(1)}, f32[4,8,256]{2,1,0:T(8,128)S(1)}, u32[]{:S(2)}, u32[]{:S(2)}) collective-permute-start(f32[4,8,256]{2,1,0:T(8,128)S(1)} %get-tuple-element.47), channel_id=1, source_target_pairs={{0,1},{1,2},{2,3},{3,4},{4,5},{5,6},{6,7},{8,9},{9,10},{10,11},{11... | collective-permute-start | bytes 98312 | tf_op jit(solution)/shard_map/ppermute | solution.py:360
  291.4 6.1 %collective-permute-start.31 = (f32[4,8,256]{2,1,0:T(8,128)S(1)}, f32[4,8,256]{2,1,0:T(8,128)S(1)}, u32[]{:S(2)}, u32[]{:S(2)}) collective-permute-start(f32[4,8,256]{2,1,0:T(8,128)S(1)} %get-tuple-element.46), channel_id=1, source_target_pairs={{1,0},{2,1},{3,2},{4,3},{5,4},{6,5},{7,6},{9,8},{10,9},{11,10},{12... | collective-permute-start | bytes 98312 | tf_op jit(solution)/shard_map/ppermute | solution.py:360
  294.6 3.0 copy-start
  297.5 0.6 copy-start.2
Sparse Core Ops, SparseCore 0:
  19.1 30.1 all-gather.2
  61.7 40.5 reduce-scatter.2
  140.3 28.5 all-gather.4
  181.3 40.8 reduce-scatter.4

commit v2 on v1

v2 whole, which is shorter than its diff:
```python
import functools
import math

import jax
import jax.numpy as jnp
from jax import lax
from jax.experimental import pallas as pl
from jax.experimental.pallas import tpu as pltpu
from jax.sharding import PartitionSpec as P

ITERS = 2
HALO = 4
EDGE = 8
LANES = 128
LEVELS = 3
STEP_PRIMAL = 0.5
STEP_DUAL = 0.5
F32 = jnp.float32
BF16 = jnp.bfloat16
VMEM = pl.BlockSpec(memory_space=pltpu.VMEM)
SMEM = pl.BlockSpec(memory_space=pltpu.SMEM)


def sincos(angle):
    turn = jnp.floor(angle * (2.0 / math.pi) + 0.5)
    rest = angle - turn * 1.5703125
    rest = rest - turn * 4.83751296997e-04
    rest = rest - turn * 7.54978995489e-08
    square = rest * rest
    sine = rest + rest * square * (
        -1.6666654611e-1 + square * (8.3321608736e-3 - square * 1.9515295891e-4)
    )
    cosine = (1.0 - 0.5 * square) + square * square * (
        4.166664568298827e-2 + square * (-1.388731625493765e-3 + square * 2.443315711809948e-5)
    )
    odd = jnp.abs(turn) == 1.0
    far = jnp.abs(turn) == 2.0
    sin_out = jnp.where(odd, turn * cosine, jnp.where(far, -sine, sine))
    cos_out = jnp.where(odd, -turn * sine, jnp.where(far, -cosine, cosine))
    return sin_out, cos_out


def root_of_unity(number, count):
    number = lax.rem(number, jnp.int32(count))
    number = jnp.where(number >= count // 2, number - count, number)
    return sincos(number.astype(F32) * (2.0 * math.pi / count))


def halves(value):
    high = value.astype(BF16)
    return high, (value - high.astype(F32)).astype(BF16)


def dot(left, right, transposed=False):
    dims = (((1,), (1 if transposed else 0,)), ((), ()))
    return lax.dot_general(left, right, dims, preferred_element_type=F32)


def dot_three(left, right_high, right_low, transposed=False):
    rows = left.shape[0]
    high, low = halves(left)
    both = dot(jnp.concatenate([high, low], axis=0), right_high, transposed)
    return both[:rows] + both[rows:] + dot(high, right_low, transposed)


def screens(phase, cos_ref, sin_ref):
    step = 16

    def screen(i, carry):
        at = pl.ds(pl.multiple_of(i * step, step), step)
        sine, cosine = sincos(phase[at, :])
        cos_ref[at, :] = cosine
        sin_ref[at, :] = sine
        return carry

    lax.fori_loop(0, phase.shape[0] // step, screen, 0)


def transforms(weight, rows_col, rows_lane, g_high, g_low, r_ref, rt_ref, slabs):
    full_rows = rt_ref.shape[0]
    full_cols, vis = weight.shape
    picked = rows_col.shape[0]
    sine, cosine = root_of_unity(
        rows_col[:, 0:1] * lax.broadcasted_iota(jnp.int32, (picked, full_rows), 1), full_rows
    )
    scale = 1.0 / math.sqrt(full_rows)
    high, low = halves(jnp.concatenate([cosine * scale, -sine * scale], axis=0))
    r_ref[...] = jnp.concatenate([high, low], axis=0)
    sine, cosine = root_of_unity(
        rows_lane[0:1, :] * lax.broadcasted_iota(jnp.int32, (full_rows, picked), 0), full_rows
    )
    high, low = halves(jnp.concatenate([cosine * scale, -sine * scale], axis=1))
    rt_ref[...] = jnp.concatenate([high, high, low], axis=1)

    half = full_cols // 2
    scale = 1.0 / math.sqrt(full_cols)
    count = vis // LANES
    for k in range(count):
        slabs[k] = weight[:, k * LANES : (k + 1) * LANES] * scale
    even_high, even_low = halves(
        jnp.concatenate([slabs[k, pl.ds(0, half, 2), :] for k in range(count)], axis=1)
    )
    odd_high, odd_low = halves(
        jnp.concatenate([slabs[k, pl.ds(1, half, 2), :] for k in range(count)], axis=1)
    )
    tile = 64

    def transform(i, carry):
        base = pl.multiple_of(i * tile, tile)
        line = base + lax.broadcasted_iota(jnp.int32, (tile, half), 0)
        cell = 2 * lax.broadcasted_iota(jnp.int32, (tile, half), 1)
        sine, cosine = root_of_unity(line * cell, full_cols)
        even = dot_three(jnp.concatenate([cosine, -sine], axis=0), even_high, even_low)
        sine, cosine = root_of_unity(line * (cell + 1), full_cols)
        odd = dot_three(jnp.concatenate([cosine, -sine], axis=0), odd_high, odd_low)
        for where, total in ((base, even + odd), (base + half, even - odd)):
            where = pl.multiple_of(where, tile)
            high, low = halves(jnp.concatenate([total[:tile], total[tile:]], axis=1))
            g_high[pl.ds(where, tile), :] = high
            g_low[pl.ds(where, tile), :] = low
        return carry

    lax.fori_loop(0, half // tile, transform, 0)


def lane_index(width):
    return lax.broadcasted_iota(jnp.int32, (1, width), 1)


def turned(value, distance):
    distance = distance % value.shape[-1]
    return value if distance == 0 else pltpu.roll(value, distance, value.ndim - 1)


def gap_of(level):
    return level + jnp.where(level == LEVELS, 1, 0)


def synthesis_body(dual, taps, levels, out, spill_right, spill_left, padded, plus, minus):
    bases, channels, rows, cols = dual.shape
    tall = rows + 2 * EDGE
    step = 16
    zeros = jnp.zeros((bases, channels, 2 * EDGE, cols), F32)
    padded[:, :, : 2 * EDGE, :] = zeros
    padded[:, :, rows + 2 * EDGE :, :] = zeros
    padded[:, :, 2 * EDGE : 2 * EDGE + rows, :] = dual[...]

    def one(i, carry):
        c = lax.rem(i, channels)
        row = pl.multiple_of(lax.div(i, channels) * step, step)
        none = jnp.zeros((step, cols), F32)
        centre, ahead, behind = none, [none] * LEVELS, [none] * LEVELS
        for q in range(bases):
            gap = gap_of(levels[q])
            block = padded[q, c, pl.ds(row, step + 2 * EDGE), :]
            value = taps[6 * q + 1] * block[EDGE : EDGE + step]
            lower = pltpu.roll(block, step + 2 * EDGE - gap, 0)
            value += taps[6 * q] * lower[EDGE : EDGE + step]
            upper = pltpu.roll(block, gap, 0)
            value += taps[6 * q + 2] * upper[EDGE : EDGE + step]
            centre += taps[6 * q + 4] * value
            for k in range(LEVELS):
                here = levels[q] == k + 1
                behind[k] += jnp.where(here, taps[6 * q + 3], 0.0) * value
                ahead[k] += jnp.where(here, taps[6 * q + 5], 0.0) * value
        out[c, pl.ds(row, step), :] = centre
        for k in range(LEVELS):
            plus[k, c, pl.ds(row, step), :] = ahead[k]
            minus[k, c, pl.ds(row, step), :] = behind[k]
        return carry

    lax.fori_loop(0, channels * (tall // step), one, 0)
    lane = lane_index(cols)
    near = lane_index(LANES)
    right = jnp.zeros((tall, LANES), F32)
    left = jnp.zeros((tall, LANES), F32)
    for c in range(channels):
        total = out[c]
        to_right = jnp.zeros((tall, LANES), F32)
        to_left = jnp.zeros((tall, LANES), F32)
        for level in range(LEVELS):
            gap = 2**level
            moved = turned(plus[level, c], gap)
            total += jnp.where(lane >= gap, moved, 0.0)
            to_right += jnp.where(near < gap, moved[:, :LANES], 0.0)
            moved = turned(minus[level, c], -gap)
            total += jnp.where(lane < cols - gap, moved, 0.0)
            to_left += jnp.where(near >= LANES - gap, moved[:, cols - LANES :], 0.0)
        out[c] = total
        right += turned(to_right, HALO * c)
        left += turned(to_left, -HALO * c)
    spill_right[...] = right
    spill_left[...] = left


def widen(tile, cols, at_end):
    if cols == LANES:
        return tile
    rest = jnp.zeros((tile.shape[0], cols - LANES), F32)
    return jnp.concatenate([rest, tile] if at_end else [tile, rest], axis=1)


def update_body(
    now, gradient, synth, side_low, side_high, top, bottom, updated, leading, pack_left, pack_right
):
    channels, rows, cols = now.shape
    near = lane_index(LANES)
    to_left = jnp.zeros((rows, LANES), F32)
    to_right = jnp.zeros((rows, LANES), F32)
    none = jnp.zeros((rows - EDGE, cols), F32)

    def folded(side):
        inside = side[EDGE : EDGE + rows, :]
        rest = jnp.zeros((rows - EDGE, LANES), F32)
        inside += jnp.concatenate([side[:EDGE, :], rest], axis=0)
        inside += jnp.concatenate([rest, side[EDGE + rows :, :]], axis=0)
        return inside

    low = folded(side_low)
    high = folded(side_high)
    for c in range(channels):
        total = synth[c, EDGE : EDGE + rows, :]
        total += jnp.concatenate([top[c], none], axis=0)
        total += jnp.concatenate([none, bottom[c]], axis=0)
        total += widen(jnp.where(near < HALO, turned(low, -HALO * c), 0.0), cols, False)
        total += widen(jnp.where(near >= LANES - HALO, turned(high, HALO * c), 0.0), cols, True)
        before = now[c]
        after = jnp.maximum(before - STEP_PRIMAL * (gradient[c] + total), 0.0)
        updated[c] = after
        ahead = 2.0 * after - before
        leading[c] = ahead
        to_left += turned(jnp.where(near < HALO, ahead[:, :LANES], 0.0), HALO * c)
        to_right += turned(
            jnp.where(near >= LANES - HALO, ahead[:, cols - LANES :], 0.0), -HALO * c
        )
    for pack, value in ((pack_left, to_left), (pack_right, to_right)):
        pack[0:EDGE, :] = value[:EDGE]
        pack[EDGE : EDGE + rows, :] = value
        pack[EDGE + rows :, :] = value[rows - EDGE :]


def analysis_body(
    leading, side_low, side_high, top, bottom, dual, taps, levels, radius, out, fields
):
    bases, channels, rows, cols = dual.shape
    near = lane_index(LANES)
    for c in range(channels):
        field = jnp.concatenate([top[c], leading[c], bottom[c]], axis=0)
        before = turned(side_low, HALO * c)
        behind = turned(side_high, -HALO * c)
        fields[0, c] = field[EDGE : EDGE + rows]
        for level in range(LEVELS):
            gap = 2**level
            moved = turned(field, gap)
            first = jnp.where(near < gap, turned(before, gap), moved[:, :LANES])
            if cols > LANES:
                first = jnp.concatenate([first, moved[:, LANES:]], axis=1)
            moved = turned(field, -gap)
            last = jnp.where(near >= LANES - gap, turned(behind, -gap), moved[:, cols - LANES :])
            if cols > LANES:
                last = jnp.concatenate([moved[:, : cols - LANES], last], axis=1)
            place = 8 * level
            for down in (-gap, 0, gap):
                for shifted in (first, field, last):
                    if down or shifted is not field:
                        place += 1
                        fields[place, c] = shifted[EDGE + down : EDGE + down + rows]

    def one(i, carry):
        q = lax.div(i, rows // EDGE)
        row = pl.ds(pl.multiple_of(lax.rem(i, rows // EDGE) * EDGE, EDGE), EDGE)
        place = 8 * (jnp.clip(levels[q], 1, LEVELS) - 1)
        weights = [
            (STEP_DUAL * taps[6 * q + a]) * taps[6 * q + 3 + e] for a in range(3) for e in range(3)
        ]
        raised = []
        energy = jnp.zeros((EDGE, cols), F32)
        for c in range(channels):
            value = dual[q, c, row, :] + weights[4] * fields[0, c, row, :]
            for j, weight in enumerate(weights[:4] + weights[5:]):
                value += weight * fields[place + 1 + j, c, row, :]
            energy += value * value
            raised.append(value)
        factor = radius[q] / jnp.maximum(jnp.sqrt(energy), radius[q])
        for c in range(channels):
            out[q, c, row, :] = raised[c] * factor
        return carry

    lax.fori_loop(0, bases * (rows // EDGE), one, 0, unroll=2)


MESH = pl.DeviceIdType.MESH


def forward_chunk(block, at, cos_ref, sin_ref, g_high, g_low, r_ref, total):
    picked = r_ref.shape[0] // 4

    def rows_of(screen):
        high, low = halves(block * screen[:, at])
        both = dot(r_ref[...], high)
        return both[: 2 * picked] + both[2 * picked :] + dot(r_ref[0 : 2 * picked, :], low)

    real = rows_of(cos_ref)
    imag = rows_of(sin_ref)
    spectrum = jnp.concatenate(
        [real[:picked] - imag[picked:], imag[:picked] + real[picked:]], axis=0
    )
    total[...] += dot_three(spectrum, g_high[at, :], g_low[at, :])


def misfit_of(total, data):
    picked, vis = data.shape[1:]
    sums = total[...]
    real = sums[:picked, :vis] - sums[picked:, vis:] - data[0]
    imag = sums[:picked, vis:] + sums[picked:, :vis] - data[1]
    total[...] = jnp.concatenate(
        [jnp.concatenate([real, imag], axis=1), jnp.concatenate([imag, -real], axis=1)], axis=0
    )


def backward_chunk(misfit, at, cos_ref, sin_ref, g_high, g_low, rt_ref):
    picked = misfit.shape[0] // 2
    back = dot_three(misfit, g_high[at, :], g_low[at, :], True)
    swapped = jnp.concatenate([back[picked:], -back[:picked]], axis=0)
    high, low = halves(jnp.concatenate([back, swapped], axis=1))
    grid = dot(rt_ref[...], jnp.concatenate([high, low, high], axis=0))
    chunk = back.shape[1]
    return cos_ref[:, at] * grid[:, :chunk] + sin_ref[:, at] * grid[:, chunk:]


def whole_body(
    nc,
    nt,
    sky,
    dual,
    phase,
    rows_col,
    rows_lane,
    weight,
    data,
    taps,
    levels,
    radius,
    sky_out,
    dual_out,
    cos_ref,
    sin_ref,
    g_high,
    g_low,
    r_ref,
    rt_ref,
    slabs,
    total,
    image,
    part,
    pair,
    strip,
    summed,
    gradient,
    sky_mid,
    dual_mid,
    synth,
    padded,
    plus,
    minus,
    leading,
    fields,
    side_low,
    side_high,
    top,
    bottom,
    pack_right,
    pack_left,
    edge_top,
    edge_bottom,
    a_send,
    a_recv,
    b_send,
    b_recv,
    c_send,
    c_recv,
    p_send,
    p_recv,
    s_send,
    s_recv,
    z_send,
    z_recv,
    h_send,
    h_recv,
):
    channels, rows, cols = sky.shape
    tall = rows + 2 * EDGE
    chips = nt // 2
    c = lax.axis_index("chan")
    t = lax.axis_index("tblk")
    core = lax.rem(t, 2)
    chip = lax.div(t, 2)
    right, left = lax.rem(c + 1, nc), lax.rem(c + nc - 1, nc)
    below, above = lax.rem(t + 1, nt), lax.rem(t + nt - 1, nt)
    sibling = (c, 2 * chip + 1 - core)

    def plane(distance):
        return 2 * lax.rem(chip + distance, chips) + core

    partners = [(lax.rem(c + d, nc), t) for d in range(1, nc)]
    partners += [(c, plane(d)) for d in range(1, chips)]
    partners += [(c, below), (c, above)]
    partners += [(right, below), (right, above), (left, below), (left, above)]
    barrier = pltpu.get_barrier_semaphore()
    for partner in partners:
        pl.semaphore_signal(barrier, inc=1, device_id=partner, device_id_type=MESH)
    pl.semaphore_wait(barrier, len(partners))

    def remote(src, dst, send, recv, device):
        return pltpu.make_async_remote_copy(
            src_ref=src,
            dst_ref=dst,
            send_sem=send,
            recv_sem=recv,
            device_id=device,
            device_id_type=MESH,
        )

    def strip_of(owner):
        return pl.ds(pl.multiple_of(owner * rows, rows), rows)

    def column(k):
        return lax.rem(c + k, nc)

    def tile_to_channel(it, source, k):
        target = column(k)
        return remote(
            source.at[target],
            image.at[it, c, strip_of(t), :],
            a_send.at[it, k],
            a_recv.at[it, nc - k],
            (target, t),
        )

    def tile_from_channel(it, source, k):
        other = column(k)
        return remote(
            source.at[other],
            image.at[it, other, strip_of(t), :],
            a_send.at[it, k],
            a_recv.at[it, k],
            (other, t),
        )

    def tile_to_chip(it, d, k):
        where = image.at[it, column(k), strip_of(t), :]
        return remote(
            where, where, b_send.at[it, d - 1, k], b_recv.at[it, d - 1, k], (c, plane(d))
        )

    def tile_to_sibling(it, d, k):
        where = image.at[it, column(k), strip_of(plane(chips - d)), :]
        return remote(where, where, c_send.at[it, d, k], c_recv.at[it, d, k], sibling)

    def half_to_sibling(it, k):
        return remote(
            part.at[k, 1 - core], pair.at[it, k], p_send.at[it, k], p_recv.at[it, k], sibling
        )

    def strip_to_chip(it, d, k):
        return remote(
            part.at[k, core, lax.rem(chip + d, chips)],
            strip.at[it, d - 1, k],
            s_send.at[it, d - 1, k],
            s_recv.at[it, d - 1, k],
            (c, plane(d)),
        )

    def tile_to_facet(it, k):
        target = column(k)
        return remote(
            summed.at[it, k],
            gradient.at[it, c],
            z_send.at[it, k],
            z_recv.at[it, nc - k],
            (target, t),
        )

    def tile_from_facet(it, k):
        other = column(k)
        return remote(
            summed.at[it, k],
            gradient.at[it, other],
            z_send.at[it, k],
            z_recv.at[it, k],
            (other, t),
        )

    first, middle, last = pl.ds(0, EDGE), pl.ds(EDGE, rows), pl.ds(EDGE + rows, EDGE)

    def edges(stage):
        routes = [
            (pack_right.at[stage, middle], side_low.at[stage, middle], (right, t)),
            (pack_right.at[stage, last], side_low.at[stage, first], (right, below)),
            (pack_right.at[stage, first], side_low.at[stage, last], (right, above)),
            (pack_left.at[stage, middle], side_high.at[stage, middle], (left, t)),
            (pack_left.at[stage, last], side_high.at[stage, first], (left, below)),
            (pack_left.at[stage, first], side_high.at[stage, last], (left, above)),
            (edge_bottom.at[stage], top.at[stage], (c, below)),
            (edge_top.at[stage], bottom.at[stage], (c, above)),
        ]
        return [
            remote(src, dst, h_send.at[stage, i], h_recv.at[stage, i], device)
            for i, (src, dst, device) in enumerate(routes)
        ]

    def kept(flag, value):
        return jnp.where(flag, value, jnp.zeros_like(value))

    def side_of(ref, stage, inside):
        return jnp.concatenate(
            [
                kept(inside & (t > 0), ref[stage, 0:EDGE, :]),
                kept(inside, ref[stage, EDGE : EDGE + rows, :]),
                kept(inside & (t < nt - 1), ref[stage, EDGE + rows :, :]),
            ],
            axis=0,
        )

    def arrived(stage):
        for copy in edges(stage):
            copy.wait()
        return (
            side_of(side_low, stage, c > 0),
            side_of(side_high, stage, c < nc - 1),
            [kept(t > 0, top[stage, i]) for i in range(channels)],
            [kept(t < nt - 1, bottom[stage, i]) for i in range(channels)],
        )

    now, coefs = sky, dual
    for it in range(ITERS):
        next_sky, next_dual = (sky_out, dual_out) if it == ITERS - 1 else (sky_mid, dual_mid)
        for k in range(1, nc):
            tile_to_channel(it, now, k).start()
        image[it, c, strip_of(t), :] = now[c]
        if it == 0:
            screens(phase, cos_ref, sin_ref)
        for k in range(nc):
            if k > 0:
                tile_from_channel(it, now, k).wait_recv()
            for d in range(1, chips):
                tile_to_chip(it, d, k).start()
            tile_to_sibling(it, 0, k).start()
        if it == 0:
            transforms(weight, rows_col, rows_lane, g_high, g_low, r_ref, rt_ref, slabs)
        synthesis_body(
            coefs,
            taps,
            levels,
            synth,
            pack_right.at[2 * it],
            pack_left.at[2 * it],
            padded,
            plus,
            minus,
        )
        edge_top[2 * it] = synth[:, 0:EDGE, :]
        edge_bottom[2 * it] = synth[:, EDGE + rows :, :]
        for k in range(nc):
            for d in range(1, chips):
                tile_to_chip(it, d, k).wait_recv()
                tile_to_sibling(it, d, k).start()
        for copy in edges(2 * it):
            copy.start()

        total[...] = jnp.zeros_like(total)
        for k in range(nc):
            for d in range(chips):
                tile_to_sibling(it, d, k).wait_recv()

        def forward(k, carry):
            here = column(k)
            at = pl.ds(pl.multiple_of(here * cols, cols), cols)
            forward_chunk(image[it, here], at, cos_ref, sin_ref, g_high, g_low, r_ref, total)
            return carry

        lax.fori_loop(0, nc, forward, 0)
        misfit_of(total, data)

        def backward(step, carry):
            @pl.when(step < nc)
            def _():
                k = lax.rem(step + 1, nc)
                at = pl.ds(pl.multiple_of(column(k) * cols, cols), cols)
                value = backward_chunk(total[...], at, cos_ref, sin_ref, g_high, g_low, rt_ref)
                for owner in range(nt):
                    part[k, owner % 2, owner // 2] = value[owner * rows : (owner + 1) * rows]
                half_to_sibling(it, k).start()

            @pl.when((step >= 1) & (step <= nc))
            def _():
                k = lax.rem(step, nc)
                half_to_sibling(it, k).wait_recv()
                part[k, core] += pair[it, k]
                for d in range(1, chips):
                    strip_to_chip(it, d, k).start()

            @pl.when(step >= 2)
            def _():
                k = lax.rem(step - 1, nc)
                value = part[k, core, chip]
                for d in range(1, chips):
                    strip_to_chip(it, d, k).wait_recv()
                    value += strip[it, d - 1, k]

                @pl.when(k > 0)
                def _():
                    summed[it, k] = value
                    tile_to_facet(it, k).start()

                @pl.when(k == 0)
                def _():
                    gradient[it, c] = value

            return carry

        lax.fori_loop(0, nc + 2, backward, 0)
        low, high, up, down = arrived(2 * it)
        for k in range(1, nc):
            tile_from_facet(it, k).wait_recv()
        stage = 2 * it + 1
        update_body(
            now,
            gradient.at[it],
            synth,
            low,
            high,
            up,
            down,
            next_sky,
            leading,
            pack_left.at[stage],
            pack_right.at[stage],
        )
        edge_top[stage] = leading[:, 0:EDGE, :]
        edge_bottom[stage] = leading[:, rows - EDGE :, :]
        for copy in edges(stage):
            copy.start()
        low, high, up, down = arrived(stage)
        analysis_body(
            leading, low, high, up, down, coefs, taps, levels, radius, next_dual, fields
        )
        for k in range(nc):
            half_to_sibling(it, k).wait_send()
            for d in range(1, chips):
                tile_to_chip(it, d, k).wait_send()
                strip_to_chip(it, d, k).wait_send()
            for d in range(chips):
                tile_to_sibling(it, d, k).wait_send()
            if k > 0:
                tile_to_channel(it, now, k).wait_send()
                tile_to_facet(it, k).wait_send()
        now, coefs = next_sky, next_dual


def arr(*shape, dtype=F32):
    return jax.ShapeDtypeStruct(shape, dtype)


def per_device(sky, dual, phase, rows_at, weight, vis_data, filters, level_counts, radius):
    channels, rows, cols = sky.shape
    nc, nt = lax.axis_size("chan"), lax.axis_size("tblk")
    chips = nt // 2
    full_rows, full_cols = phase.shape[2:]
    vis = weight.shape[3]
    picked = rows_at.shape[2]
    tall = rows + 2 * EDGE
    stages = 2 * ITERS
    block = lambda *shape, dtype=F32: pltpu.VMEM(shape, dtype)
    scratch = [
        block(full_rows, full_cols),
        block(full_rows, full_cols),
        block(full_cols, 2 * vis, dtype=BF16),
        block(full_cols, 2 * vis, dtype=BF16),
        block(4 * picked, full_rows, dtype=BF16),
        block(full_rows, 6 * picked, dtype=BF16),
        block(vis // LANES, full_cols, LANES),
        block(2 * picked, 2 * vis),
        block(ITERS, nc, full_rows, cols),
        block(nc, 2, chips, rows, cols),
        block(ITERS, nc, chips, rows, cols),
        block(ITERS, chips - 1, nc, rows, cols),
        block(ITERS, nc, rows, cols),
        block(ITERS, channels, rows, cols),
        block(*sky.shape),
        block(*dual.shape),
        block(channels, tall, cols),
        block(*dual.shape[:2], rows + 4 * EDGE, cols),
        block(LEVELS, channels, tall, cols),
        block(LEVELS, channels, tall, cols),
        block(*sky.shape),
        block(1 + 8 * LEVELS, channels, rows, cols),
        block(stages, tall, LANES),
        block(stages, tall, LANES),
        block(stages, channels, EDGE, cols),
        block(stages, channels, EDGE, cols),
        block(stages, tall, LANES),
        block(stages, tall, LANES),
        block(stages, channels, EDGE, cols),
        block(stages, channels, EDGE, cols),
    ]
    for shape in (
        (ITERS, nc),
        (ITERS, chips - 1, nc),
        (ITERS, chips, nc),
        (ITERS, nc),
        (ITERS, chips - 1, nc),
        (ITERS, nc),
        (stages, 8),
    ):
        scratch += [pltpu.SemaphoreType.DMA(shape)] * 2
    return pl.pallas_call(
        functools.partial(whole_body, nc, nt),
        out_shape=(arr(*sky.shape), arr(*dual.shape)),
        in_specs=[VMEM] * 7 + [SMEM] * 3,
        out_specs=(VMEM, VMEM),
        scratch_shapes=scratch,
        compiler_params=pltpu.CompilerParams(
            vmem_limit_bytes=60 * 1024 * 1024, collective_id=0, has_side_effects=True
        ),
        name="primal_dual",
    )(
        sky,
        dual,
        phase[0, 0],
        rows_at[0, 0][:, None],
        rows_at[0, 0][None, :],
        weight[0, 0],
        vis_data[0, 0],
        filters.reshape(-1),
        level_counts,
        radius,
    )


def solution(mesh):
    placed = (
        P(None, "tblk", "chan"),
        P(None, None, "tblk", "chan"),
        P("chan", "tblk", None, None),
        P("chan", "tblk", None),
        P("chan", "tblk", None, None),
        P("chan", "tblk", None, None, None),
        P(),
        P(),
        P(),
    )
    return jax.shard_map(
        per_device,
        mesh=mesh,
        in_specs=placed,
        out_specs=(P(None, "tblk", "chan"), P(None, None, "tblk", "chan")),
        check_vma=False,
    )
```

time: 314 us -> 119 us (0.38)
  starting transfers between devices: 105 us -> 0 us
  waiting for transfers between devices: 65.5 us -> 0 us
  Pallas kernels: 66.4 us -> 110 us
  blocking collectives: 22.4 us -> 0 us
  local copies, waits for them, and re-layouts: 26.2 us -> 7.74 us
  between operations: 14.2 us -> 0.64 us
  other arithmetic: 11.7 us -> 0 us
    ppermute x32 -> x0, starting transfers between devices: 96.6 us -> none  [neighbour(): return lax.ppermute(value, ('chan', 'tblk'), route)]
    all_gather x2 -> x0, waiting for transfers between devices: 43.4 us -> none  [per_device(): whole = lax.all_gather(spread[0], 'tblk', axis=0, tiled=True)]
    pallas_call x9 -> x1, Pallas kernels: 66.4 us -> 110 us  [per_device(): pl.pallas_call(functools.partial(whole_body, nc, nt), out_shape=(arr(*sky...]
    all_to_all x2 -> x0, blocking collectives: 22.4 us -> none  [per_device(): lax.all_to_all(sky, 'chan', split_axis=0, concat_axis=2, tiled=True)]
    reduce_scatter x2 -> x0, waiting for transfers between devices: 16 us -> none  [per_device(): summed = lax.psum_scatter(part, 'tblk', scatter_dimension=0, tiled=True)]
    slice x16 -> x0, local copies, waits for them, and re-layouts: 10.3 us -> none  [the longest x4 3.07 us: per_device(): spill[EDGE:EDGE + rows]]
    all_to_all x2 -> x0, starting transfers between devices: 7.98 us -> none  [per_device(): lax.all_to_all(summed[None], 'chan', split_axis=2, concat_axis=0, tiled=T...]
    ppermute x32 -> x0, waiting for transfers between devices: 6.04 us -> none  [neighbour(): return lax.ppermute(value, ('chan', 'tblk'), route)]
  transfers between devices with their start and end apart: 38 -> 0, of which waited for: 5 -> 0; matrix products, arithmetic and copies ran while one was open for 10% -> 0% of each run, Pallas kernels for 10% -> 0%
where the time goes in v2:
time: 119 us; the launch traced here: 118 us
  Pallas kernels  110 us (92%)
  local copies, waits for them, and re-layouts  7.74 us (7%)
    pallas_call x1, Pallas kernels, per_device(): pl.pallas_call(functools.partial(whole_body, nc, nt), out_shape=(arr(*sky...  110 us
    unnamed x3, local copies, waits for them, and re-layouts  5.78 us

profile of v2, /device:TPU:11, one launch (start us, length us, event | category | flops | bytes accessed | tf_op | source)
XLA Modules:
  0.0 118.1 jit_solution(5251306389822162645)
XLA Ops:
  0.6 0.8 copy.13
  1.4 0.6 reshape.7.taps
  2.0 1.4 %copy.14.rows_col = s32[64,1]{1,0:T(8,128)} copy(s32[64,1]{0,1:T(1,128)} %bitcast.8) | data formatting | bytes 512 | tf_op jit(solution)/shard_map/broadcast_in_dim;squeeze | solution.py:731
  3.4 109.7 %primal_dual.1 = (f32[4,64,256]{2,1,0:T(8,128)}, f32[9,4,64,256]{3,2,1,0:T(8,128)}) custom-call(f32[4,64,256]{2,1,0:T(8,128)} %sky.1, f32[9,4,64,256]{3,2,1,0:T(8,128)} %dual.1, f32[512,1024]{1,0:T(8,128)} %bitcast.5, s32[64,1]{1,0:T(8,128)} %copy.14.rows_col, s32[1,64]{1,0:T(1,128)} %bitcast.9, f32[1024,256]{1,0:T(8,128)} %bitcast.6, ...), custom_call_target="tpu_custom_call" | custom-call | tf_op jit(solution)/shard_map/primal_dual/pallas_call | solution.py:717
  113.1 1.7 %copy.17 = f32[4,64,256]{2,1,0:T(8,128)} copy(f32[4,64,256]{2,1,0:T(8,128)} %get-tuple-element.4) | data formatting | bytes 524288
  114.8 3.3 %copy.18 = f32[9,4,64,256]{3,2,1,0:T(8,128)} copy(f32[9,4,64,256]{3,2,1,0:T(8,128)} %get-tuple-element.5) | data formatting | bytes 4718592

commit v3 on v2

--- a/solution.py
+++ b/solution.py
@@ -538,14 +538,14 @@
         for k in range(1, nc):
             tile_to_channel(it, now, k).start()
         image[it, c, strip_of(t), :] = now[c]
-        if it == 0:
-            screens(phase, cos_ref, sin_ref)
         for k in range(nc):
             if k > 0:
                 tile_from_channel(it, now, k).wait_recv()
             for d in range(1, chips):
                 tile_to_chip(it, d, k).start()
             tile_to_sibling(it, 0, k).start()
+            if it == 0 and k == 0:
+                screens(phase, cos_ref, sin_ref)
         if it == 0:
             transforms(weight, rows_col, rows_lane, g_high, g_low, r_ref, rt_ref, slabs)
         synthesis_body(
@@ -561,25 +561,29 @@
         )
         edge_top[2 * it] = synth[:, 0:EDGE, :]
         edge_bottom[2 * it] = synth[:, EDGE + rows :, :]
-        for k in range(nc):
-            for d in range(1, chips):
-                tile_to_chip(it, d, k).wait_recv()
-                tile_to_sibling(it, d, k).start()
         for copy in edges(2 * it):
             copy.start()
-
         total[...] = jnp.zeros_like(total)
-        for k in range(nc):
-            for d in range(chips):
-                tile_to_sibling(it, d, k).wait_recv()
-
-        def forward(k, carry):
-            here = column(k)
-            at = pl.ds(pl.multiple_of(here * cols, cols), cols)
-            forward_chunk(image[it, here], at, cos_ref, sin_ref, g_high, g_low, r_ref, total)
+
+        def forward(step, carry):
+            @pl.when(step < nc)
+            def _():
+                for d in range(1, chips):
+                    tile_to_chip(it, d, step).wait_recv()
+                    tile_to_sibling(it, d, step).start()
+
+            @pl.when(step >= 1)
+            def _():
+                k = step - 1
+                for d in range(chips):
+                    tile_to_sibling(it, d, k).wait_recv()
+                here = column(k)
+                at = pl.ds(pl.multiple_of(here * cols, cols), cols)
+                forward_chunk(image[it, here], at, cos_ref, sin_ref, g_high, g_low, r_ref, total)
+
             return carry
 
-        lax.fori_loop(0, nc, forward, 0)
+        lax.fori_loop(0, nc + 1, forward, 0)
         misfit_of(total, data)
 
         def backward(step, carry):

time: 119 us -> 117 us (0.983)
  Pallas kernels: 110 us -> 108 us
    pallas_call x1, Pallas kernels: 110 us -> 108 us  [per_device(): pl.pallas_call(functools.partial(whole_body, nc, nt), out_shape=(arr(*sky...]
where the time goes in v3:
time: 117 us
  Pallas kernels  108 us (92%)
  local copies, waits for them, and re-layouts  7.74 us (7%)
    pallas_call x1, Pallas kernels, per_device(): pl.pallas_call(functools.partial(whole_body, nc, nt), out_shape=(arr(*sky...  108 us
    unnamed x3, local copies, waits for them, and re-layouts  5.78 us

profile of v3, /device:TPU:11, one launch (start us, length us, event | category | flops | bytes accessed | tf_op | source)
XLA Modules:
  0.0 116.8 jit_solution(7095940010128132355)
XLA Ops:
  0.6 0.8 copy.13
  1.4 0.6 reshape.7.taps
  2.0 1.4 %copy.14.rows_col = s32[64,1]{1,0:T(8,128)} copy(s32[64,1]{0,1:T(1,128)} %bitcast.8) | data formatting | bytes 512 | tf_op jit(solution)/shard_map/broadcast_in_dim;squeeze | solution.py:735
  3.4 108.4 %primal_dual.1 = (f32[4,64,256]{2,1,0:T(8,128)}, f32[9,4,64,256]{3,2,1,0:T(8,128)}) custom-call(f32[4,64,256]{2,1,0:T(8,128)} %sky.1, f32[9,4,64,256]{3,2,1,0:T(8,128)} %dual.1, f32[512,1024]{1,0:T(8,128)} %bitcast.5, s32[64,1]{1,0:T(8,128)} %copy.14.rows_col, s32[1,64]{1,0:T(1,128)} %bitcast.9, f32[1024,256]{1,0:T(8,128)} %bitcast.6, ...), custom_call_target="tpu_custom_call" | custom-call | tf_op jit(solution)/shard_map/primal_dual/pallas_call | solution.py:721
  111.8 1.7 %copy.17 = f32[4,64,256]{2,1,0:T(8,128)} copy(f32[4,64,256]{2,1,0:T(8,128)} %get-tuple-element.4) | data formatting | bytes 524288
  113.5 3.3 %copy.18 = f32[9,4,64,256]{3,2,1,0:T(8,128)} copy(f32[9,4,64,256]{3,2,1,0:T(8,128)} %get-tuple-element.5) | data formatting | bytes 4718592
